TPU v7x, 32 devices: a whole 2x2x4 slice. The times are simulated.
32 devices in a mesh: row: 4 (over z), col: 8 (over y, x, core).
Axes of the slice: x: 2, y: 2, z: 4, core: 2. Of those that a mesh axis runs over, the one named last changes fastest.
Arguments:
- points: bfloat16 [2, 8192], P(None, ('row', 'col')), may hold values from 0 to 1
- noise_var: float32 [8192], P(('row', 'col')), may hold values from 0.5 to 2
- district: int32 [8192], P(('row', 'col')), may hold values from 0 to 63, never falling along the last dimension, each value on 1 to 512 neighbouring positions
- solution: float32 [32, 8192], P(None, ('row', 'col')), may hold values from -6 to 6
- residual: float32 [32, 8192], P(None, ('row', 'col')), may hold values from -44 to 44
- direction: float32 [32, 8192], P(None, ('row', 'col')), may hold values from -44 to 44
Outputs:
- new_solution: float32 [32, 8192], P(None, ('row', 'col'))
- new_residual: float32 [32, 8192], P(None, ('row', 'col'))
- new_direction: float32 [32, 8192], P(None, ('row', 'col'))
Inputs may be any that keep to these rules, and one draw needn't show every extreme that they name: Samples are ordered by district; every district holds 1 to 512 samples and one holds exactly 512.
All inputs are finite; a program needn't handle non-finite values.
Results may differ from a plain program's by a relative error of at most 0.004.
Values may be sent and summed in bfloat16 or wider, within the bound.
No kernel may reach another device: no remote copies, remote signals or barrier semaphores. Data moves between devices by JAX's collectives and lax.ppermute only.
A program may use at most 64 MiB of HBM per device.

v0:
```python
import math

import jax
import jax.numpy as jnp
from jax import lax
from jax.sharding import PartitionSpec as P

NDIST = 64


root_three = math.sqrt(3.0)
corr_range = 0.05
district_gain = 0.5


def matern_tile(left_points, right_points):
    left_vals = left_points.astype(jnp.float32)
    right_vals = right_points.astype(jnp.float32)
    delta_x = left_vals[0][:, None] - right_vals[0][None, :]
    delta_y = left_vals[1][:, None] - right_vals[1][None, :]
    scaled = root_three / corr_range * jnp.sqrt(delta_x * delta_x + delta_y * delta_y)
    return ((1.0 + scaled) * jnp.exp(-scaled)).astype(jnp.bfloat16)


def small_product(left, right):
    return jnp.dot(left, right, precision=lax.Precision.HIGHEST, preferred_element_type=jnp.float32)


def chol_solve(matrix, rhs_mat):
    factor = jnp.linalg.cholesky(matrix)
    return jax.scipy.linalg.cho_solve((factor, True), rhs_mat)


def per_device(points, noise_var, district, solution, residual, direction):
    local_count = points.shape[1]
    rhs_count = direction.shape[0]
    whole_count = local_count * lax.axis_size("row") * lax.axis_size("col")
    kernel_scale = 1.0 / (corr_range * math.sqrt(whole_count))
    labels = jnp.arange(NDIST, dtype=jnp.int32)
    onehot = (district[None, :] == labels[:, None]).astype(jnp.float32)
    local_sums = small_product(direction, onehot.T)
    local_sizes = jnp.sum(onehot, axis=1)
    local_norm = small_product(residual, residual.T)
    district_sums, sizes = lax.psum((local_sums, local_sizes), ("row", "col"))
    old_norm = lax.psum(local_norm, ("row", "col"))
    lowered = direction.astype(jnp.bfloat16)
    empty = jnp.zeros((rhs_count, local_count), jnp.float32)
    left_points = lax.all_gather(points, ("row", "col"), axis=1, tiled=True)
    left_dir = lax.all_gather(lowered, ("row", "col"), axis=1, tiled=True)
    width_now = left_points.shape[1]
    block_len = 8192

    def one_step(index_now, acc):
        part_points = lax.dynamic_slice_in_dim(left_points, index_now * block_len, block_len, 1)
        part_dir = lax.dynamic_slice_in_dim(left_dir, index_now * block_len, block_len, 1)
        return acc + jnp.dot(
            part_dir, matern_tile(part_points, points), preferred_element_type=jnp.float32
        )

    kernel_part = lax.fori_loop(0, width_now // block_len, one_step, empty)
    weights = district_sums / jnp.sqrt(sizes)[None, :]
    district_part = small_product(weights, onehot)
    image = (
        noise_var[None, :] * direction + kernel_part * kernel_scale + district_gain * district_part
    )
    local_curv = small_product(direction, image.T)
    curvature = lax.psum(local_curv, ("row", "col"))
    alpha = chol_solve(curvature, old_norm)
    new_solution = solution + small_product(alpha.T, direction)
    new_residual = residual - small_product(alpha.T, image)
    new_norm = lax.psum(small_product(new_residual, new_residual.T), ("row", "col"))
    beta = chol_solve(old_norm, new_norm)
    new_direction = new_residual + small_product(beta.T, direction)
    return (new_solution, new_residual, new_direction)


def solution(mesh):
    in_specs = (
        P(None, ("row", "col")),
        P(("row", "col")),
        P(("row", "col")),
        P(None, ("row", "col")),
        P(None, ("row", "col")),
        P(None, ("row", "col")),
    )
    out_specs = (P(None, ("row", "col")), P(None, ("row", "col")), P(None, ("row", "col")))
    return jax.shard_map(
        per_device, mesh=mesh, in_specs=in_specs, out_specs=out_specs, check_vma=False
    )
```

profile of v0, /device:TPU:0, one launch (start us, length us, event | category | flops | bytes accessed | tf_op | source)
XLA Modules:
  0.0 224.7 jit_solution(12056123770513564116)
XLA Ops:
  0.6 0.0 copy-start
  0.6 0.0 copy-start.5
  0.7 43.5 %all_gather.6 = bf16[2,8192]{1,0:T(2,128)(2,1)S(1)} all-gather(bf16[2,256]{1,0:T(2,128)(2,1)} %param.9), channel_id=1, replica_groups=mesh['row'=4,'col'=8] {'row','col'}, dimensions={1}, use_global_device_ids=true | all-gather | bytes 33792 | tf_op jit(solution)/shard_map/all_gather | solution.py:48
  44.2 0.8 fusion.24
  45.0 0.8 convert_element_type.21
  45.7 38.0 %all_gather.7 = bf16[32,8192]{1,0:T(8,128)(2,1)S(1)} all-gather(bf16[32,256]{1,0:T(8,128)(2,1)S(1)} %convert_element_type.21), channel_id=1, replica_groups=mesh['row'=4,'col'=8] {'row','col'}, dimensions={1}, use_global_device_ids=true | all-gather | bytes 540672 | tf_op jit(solution)/shard_map/all_gather | solution.py:49
  83.8 0.0 copy-done
  83.8 0.0 copy-done.5
  83.8 0.0 copy-start.4
  83.8 0.0 copy-start.2
  83.8 5.2 %fusion.4 = f32[32,256]{1,0:T(8,128)S(1)} fusion(bf16[32,8192]{1,0:T(8,128)(2,1)S(1)} %all_gather.7, f32[256]{0:T(256)S(1)} %bitcast.55, f32[8192]{0:T(1024)S(1)} %bitcast.53, f32[256]{0:T(256)S(1)} %bitcast.54, f32[8192]{0:T(1024)S(1)} %bitcast.52, f32[32,256]{1,0:T(8,128)S(1)} %copy-done, f32[256]{0:T(256)S(1)} %copy-done.5), kind=kOutput, calls=%fused_computation.10 | convolution fusion | flops 155213824 | bytes 658432 | tf_op jit(solution)/shard_map/while/body/eval_jaxpr/dot_general | solution.py:56
  89.0 0.0 copy-done.4
  89.0 0.2 convolution_bitcast_fusion
  89.2 0.1 convert_reduce_fusion
  89.3 37.4 %all-reduce.1 = (f32[32,64]{0,1:T(8,128)S(1)}, f32[64]{0:T(128)S(1)}) all-reduce(f32[32,64]{0,1:T(8,128)S(1)} %convolution_bitcast_fusion, f32[64]{0:T(128)S(1)} %convert_reduce_fusion), channel_id=1, replica_groups=mesh['row'=4,'col'=8] {'row','col'}, use_global_device_ids=true, to_apply=%region_0.0 | all-reduce | flops 2112 | bytes 16896 | tf_op jit(solution)/shard_map/psum | solution.py:44
  126.6 0.3 fusion.1
  126.9 0.0 copy-start.3
  127.0 0.2 convolution_bitcast_fusion.1
  127.1 0.0 copy-done.2
  127.1 0.2 fusion.25
  127.3 42.7 %all-reduce = (f32[32,32]{0,1:T(8,128)S(1)}, f32[32,32]{0,1:T(8,128)S(1)}) all-reduce(f32[32,32]{0,1:T(8,128)S(1)} %fusion.25, f32[32,32]{0,1:T(8,128)S(1)} %convolution_bitcast_fusion.1), channel_id=1, replica_groups=mesh['row'=4,'col'=8] {'row','col'}, use_global_device_ids=true, to_apply=%region_6.8 | all-reduce | flops 2048 | bytes 16384 | tf_op jit(solution)/shard_map/psum | solution.py:45
  170.0 0.1 copy.14
  170.0 0.1 copy.12
  170.1 2.9 %cholesky.55 = f32[32,32]{1,0:T(8,128)S(1)} custom-call(f32[32,32]{1,0:T(8,128)S(1)} %get-tuple-element.31), custom_call_target="Cholesky" | custom-call | tf_op jit(solution)/shard_map/jit(cholesky)/cholesky | solution.py:30
  173.1 0.6 compare_reduce_fusion
  173.7 0.7 fusion.9
  174.4 2.4 %custom-call.9 = f32[1,32,32]{1,2,0:T(8,128)S(1)} custom-call(f32[1,32,32]{2,1,0:T(8,128)S(1)} %fusion.9), custom_call_target="InvertDiagBlocksLowerTriangular" | custom-call | tf_op jit(solution)/shard_map/jit(_cho_solve)/triangular_solve | solution.py:31
  176.8 2.9 %cholesky.44 = f32[32,32]{1,0:T(8,128)S(1)} custom-call(f32[32,32]{1,0:T(8,128)S(1)} %get-tuple-element.32), custom_call_target="Cholesky" | custom-call | tf_op jit(solution)/shard_map/jit(cholesky)/cholesky | solution.py:30
  179.8 0.6 compare_reduce_fusion.1
  180.4 0.7 fusion.8
  181.1 2.4 %custom-call.8 = f32[1,32,32]{1,2,0:T(8,128)S(1)} custom-call(f32[1,32,32]{2,1,0:T(8,128)S(1)} %fusion.8), custom_call_target="InvertDiagBlocksLowerTriangular" | custom-call | tf_op jit(solution)/shard_map/jit(_cho_solve)/triangular_solve | solution.py:31
  183.5 0.2 fusion.17
  183.7 0.1 fusion.15
  183.9 0.2 convolution_subtract_fusion
  184.1 0.0 copy-start.1
  184.2 0.2 fusion.26
  184.3 38.4 %psum.39 = f32[32,32]{1,0:T(8,128)S(1)} all-reduce(f32[32,32]{1,0:T(8,128)S(1)} %fusion.26), channel_id=1, replica_groups=mesh['row'=4,'col'=8] {'row','col'}, use_global_device_ids=true, to_apply=%region_7.0 | all-reduce | flops 1024 | bytes 8192 | tf_op jit(solution)/shard_map/psum | solution.py:71
  222.7 0.2 fusion.12
  222.9 0.1 fusion.10
  223.0 0.9 convolution_add_fusion
  223.9 0.0 copy-done.3
  223.9 0.8 convolution_add_fusion.1
  224.7 0.0 copy-done.1
  (5 shorter events, 0.1 us)
Async XLA Ops:
  0.6 83.1 %copy-start = (f32[32,256]{1,0:T(8,128)S(1)}, f32[32,256]{1,0:T(8,128)}, u32[]{:S(2)}) copy-start(f32[32,256]{1,0:T(8,128)} %param.14) | copy-start | bytes 98308
  0.6 83.1 %copy-start.5 = (f32[256]{0:T(256)S(1)}, f32[256]{0:T(256)}, u32[]{:S(2)}) copy-start(f32[256]{0:T(256)} %param.10) | copy-start | bytes 3076
  83.8 5.2 %copy-start.4 = (s32[256]{0:T(256)S(1)}, s32[256]{0:T(256)}, u32[]{:S(2)}) copy-start(s32[256]{0:T(256)} %param.11) | copy-start | bytes 3076
  83.8 43.4 %copy-start.2 = (f32[32,256]{1,0:T(8,128)S(1)}, f32[32,256]{1,0:T(8,128)}, u32[]{:S(2)}) copy-start(f32[32,256]{1,0:T(8,128)} %param.13) | copy-start | bytes 98308
  126.9 97.0 %copy-start.3 = (f32[32,256]{1,0:T(8,128)S(1)}, f32[32,256]{1,0:T(8,128)}, u32[]{:S(2)}) copy-start(f32[32,256]{1,0:T(8,128)} %param.12) | copy-start | bytes 98308
  184.1 40.6 %copy-start.1 = (f32[32,256]{1,0:T(8,128)}, f32[32,256]{1,0:T(8,128)S(1)}, u32[]{:S(2)}) copy-start(f32[32,256]{1,0:T(8,128)S(1)} %convolution_subtract_fusion) | copy-start | bytes 98308
where the time goes:
time: 225 us
  blocking collectives  200 us (89%)
  other arithmetic  14.3 us (6%)
  matrix products  8.77 us (4%)
    all_gather x1, blocking collectives, per_device(): left_points = lax.all_gather(points, ('row', 'col'), axis=1, tiled=True)  43.5 us
    psum x1, blocking collectives, per_device(): old_norm = lax.psum(local_norm, ('row', 'col'))  42.7 us
    psum x1, blocking collectives, per_device(): lax.psum(small_product(new_residual, new_residual.T), ('row', 'col'))  38.4 us
    all_gather x1, blocking collectives, per_device(): left_dir = lax.all_gather(lowered, ('row', 'col'), axis=1, tiled=True)  38 us
    psum x1, blocking collectives, per_device(): district_sums, sizes = lax.psum((local_sums, local_sizes), ('row', 'col'))  37.4 us
    another operation x6, other arithmetic, chol_solve(): factor = jnp.linalg.cholesky(matrix)  7.2 us
    another operation x4, other arithmetic, chol_solve(): return jax.scipy.linalg.cho_solve((factor, True), rhs_mat)  6.17 us
    dot_general x1, matrix products, one_step(): jnp.dot(part_dir, matern_tile(part_points, points), preferred_element_typ...  5.2 us

commit v1 on v0

v1 whole, which is shorter than its diff:
```python
import functools
import math

import jax
import jax.numpy as jnp
from jax import lax
from jax.experimental import pallas as pl
from jax.experimental.pallas import tpu as pltpu
from jax.sharding import Mesh, PartitionSpec as P

root_three = math.sqrt(3.0)
corr_range = 0.05
district_gain = 0.5
LANES = 128
ROWS = 72
F32, BF16 = jnp.float32, jnp.bfloat16


def dot_f32(left, right, dims):
    return lax.dot_general(
        left, right, (dims, ((), ())), precision=lax.Precision.HIGHEST, preferred_element_type=F32
    )


def dot_bf16(left, right, dims):
    return lax.dot_general(left, right, (dims, ((), ())), preferred_element_type=F32)


def three_pieces(vals):
    high = vals.astype(BF16)
    rest = vals - high.astype(F32)
    mid = rest.astype(BF16)
    low = (rest - mid.astype(F32)).astype(BF16)
    return high, mid, low


def pack_kernel(copies, points_ref, dist_ref, dir_ref, res_ref, pack_ref, own_ref, norm_ref):
    count = dir_ref.shape[1]
    rhs = dir_ref.shape[0]
    direction = dir_ref[...]
    dist = dist_ref[...]
    high, mid, low = three_pieces(direction)
    pad = jnp.zeros((LANES - 3 * rhs, count), BF16)
    ones = jnp.ones((LANES - 3 * rhs, count), BF16)
    stacked = jnp.concatenate([high, mid, low, ones], axis=0)
    labels = lax.broadcasted_iota(jnp.int32, (64, count), 0)
    onehot = (labels == dist).astype(F32).astype(BF16)
    same = dot_bf16(onehot, onehot, ((0,), (0,))).astype(BF16)
    sums = dot_bf16(stacked, same, ((1,), (0,)))
    own = sums[0:rhs] + sums[rhs : 2 * rhs] + sums[2 * rhs : 3 * rhs]
    own_ref[0:rhs, :] = own
    own_ref[rhs:, :] = sums[3 * rhs : 3 * rhs + 8]
    first = dist[:, 0:1]
    last = dist[:, count - 1 : count]
    row = lax.broadcasted_iota(jnp.int32, (8, count), 0)
    picked = jnp.where(row == 0, first, last)
    wanted = (row == 0) | ((row == 1) & (first != last))
    mask = (wanted & (dist == picked)).astype(F32).astype(BF16)
    edge = dot_bf16(mask, stacked, ((1,), (1,)))
    total = edge + pltpu.roll(edge, LANES - rhs, 1) + pltpu.roll(edge, LANES - 2 * rhs, 1)
    lane = lax.broadcasted_iota(jnp.int32, (8, LANES), 1)
    total = jnp.where(lane < rhs, total, 0.0)
    e_high, e_mid, e_low = three_pieces(total)
    row8 = lax.broadcasted_iota(jnp.int32, (8, LANES), 0)
    label = jnp.where(row8 == 0, first, last).astype(F32)
    extras = (
        e_high.astype(F32)
        + pltpu.roll(e_mid.astype(F32), rhs, 1)
        + pltpu.roll(e_low.astype(F32), 2 * rhs, 1)
    )
    extras = jnp.where(lane == 3 * rhs, label, extras)
    extras = jnp.where(lane == 3 * rhs + 1, edge, extras)
    pts = points_ref[...].astype(F32)
    tail = jnp.concatenate(
        [pts[:, 0:LANES], pts[:, LANES:], extras[0:2, :], jnp.zeros((2, LANES), F32)], axis=0
    )
    lowered = direction.astype(BF16)
    block = jnp.concatenate(
        [lowered[:, 0:LANES].astype(F32), lowered[:, LANES:].astype(F32), tail], axis=0
    ).astype(BF16)
    for n in range(copies):
        pack_ref[n] = block
    norm_ref[...] = dot_f32(res_ref[...], res_ref[...], ((1,), (1,)))


def pack(copies, points, district, direction, residual):
    rhs, count = direction.shape
    return pl.pallas_call(
        functools.partial(pack_kernel, copies),
        out_shape=(
            jax.ShapeDtypeStruct((copies, ROWS, LANES), BF16),
            jax.ShapeDtypeStruct((rhs + 8, count), F32),
            jax.ShapeDtypeStruct((rhs, rhs), F32),
        ),
        name="pack",
    )(points, district.reshape(1, count), direction, residual)


def half_product(skip, points_ref, dist_ref, all_ref, own_x, own_y):
    blocks = all_ref.shape[0]
    count = dist_ref.shape[1]
    rhs = 32
    scale = root_three / corr_range
    pts = points_ref[...].astype(BF16)
    row = lax.broadcasted_iota(jnp.int32, (2, LANES), 0)
    own_x[...] = dot_bf16(pts, (row == 0).astype(F32).astype(BF16), ((0,), (0,))) * scale
    own_y[...] = dot_bf16(pts, (row == 1).astype(F32).astype(BF16), ((0,), (0,))) * scale

    def one_block(index, acc):
        block = all_ref[index]
        tail = block[64:72, :].astype(F32) * scale
        halves = []
        for half in range(2):
            right_x = tail[2 * half : 2 * half + 1, :]
            right_y = tail[2 * half + 1 : 2 * half + 2, :]
            parts = []
            step = 64
            for start in range(0, count, step):
                dx = own_x[start : start + step, :] - right_x
                dy = own_y[start : start + step, :] - right_y
                square = jnp.maximum(dx * dx + dy * dy, 1e-30)
                scaled = square * lax.rsqrt(square)
                parts.append(((1.0 + scaled) * jnp.exp(-scaled)).astype(BF16))
            halves.append(jnp.concatenate(parts, axis=0))
        tile = jnp.concatenate(halves, axis=1)
        left = jnp.concatenate([block[0:rhs, :], block[rhs : 2 * rhs, :]], axis=1)
        return acc + dot_bf16(left, tile, ((1,), (1,)))

    product = lax.fori_loop(0, blocks, one_block, jnp.zeros((rhs, count), F32))

    edges = all_ref[:, 64:72, :].astype(F32).reshape(blocks * 8, LANES)
    place = lax.broadcasted_iota(jnp.int32, (blocks * 8, count), 0)
    kind = place % 8
    good = ((kind == 4) | (kind == 5)) & (place // 8 != skip)
    match = good & (edges[:, 3 * rhs : 3 * rhs + 1] == dist_ref[...].astype(F32))
    sums = dot_bf16(edges.astype(BF16), match.astype(F32).astype(BF16), ((0,), (0,)))
    extra = sums[0:rhs] + sums[rhs : 2 * rhs] + sums[2 * rhs : 3 * rhs]
    return product, extra, sums[3 * rhs : 3 * rhs + 8]


def first_kernel(where_ref, points_ref, dist_ref, own_ref, all_ref, product_ref, sums_ref, own_x, own_y):
    product, extra, number = half_product(where_ref[0], points_ref, dist_ref, all_ref, own_x, own_y)
    product_ref[...] = product
    sums_ref[0:32, :] = own_ref[0:32, :] + extra
    sums_ref[32:40, :] = own_ref[32:40, :]
    sums_ref[32:33, :] = own_ref[32:33, :] + number[1:2, :]


def second_kernel(
    whole_count, points_ref, dist_ref, noise_ref, dir_ref, res_ref, norm_ref, product_ref, sums_ref, all_ref,
    image_ref, gram_ref, own_x, own_y,
):
    product, extra, number = half_product(-1, points_ref, dist_ref, all_ref, own_x, own_y)
    product = product + product_ref[...]
    size = sums_ref[32:33, :] + number[1:2, :]
    district_part = (sums_ref[0:32, :] + extra) / jnp.sqrt(size)
    direction = dir_ref[...]
    kernel_scale = 1.0 / (corr_range * math.sqrt(whole_count))
    image = noise_ref[...] * direction + product * kernel_scale + district_gain * district_part
    image_ref[...] = image
    right = jnp.concatenate([direction, res_ref[...], image], axis=0)
    gram_ref[:, 0:96] = dot_f32(image, right, ((1,), (1,)))
    gram_ref[:, 96:128] = norm_ref[...]


def final_kernel(gram_ref, sol_ref, res_ref, dir_ref, image_ref, new_sol_ref, new_res_ref, new_dir_ref):
    rhs = 32
    total = gram_ref[0]
    for n in range(1, gram_ref.shape[0]):
        total = total + gram_ref[n]
    curv = total[:, 0:32]
    cross = total[:, 32:64]
    gram_image = total[:, 64:96]
    old_norm = total[:, 96:128]
    curv = 0.5 * (curv + curv.T)
    row = lax.broadcasted_iota(jnp.int32, (rhs, rhs), 0)
    col = lax.broadcasted_iota(jnp.int32, (rhs, rhs), 1)
    eye = (row == col).astype(F32)
    work = jnp.concatenate([curv, old_norm, old_norm, eye], axis=1)
    rows = lax.broadcasted_iota(jnp.int32, (rhs, LANES), 0)
    lanes = lax.broadcasted_iota(jnp.int32, (rhs, LANES), 1)
    left_side = lanes < 64
    for step in range(rhs):
        factor = jnp.where(left_side, work[:, step : step + 1], work[:, 64 + step : 65 + step])
        pivot_row = work[step : step + 1, :]
        pivot = jnp.where(left_side[0:1], work[step : step + 1, step : step + 1], work[step : step + 1, 64 + step : 65 + step])
        scaled_row = pivot_row / pivot
        work = jnp.where(rows == step, scaled_row, work - factor * scaled_row)
    alpha = work[:, 32:64]
    norm_inverse = work[:, 96:128]
    across = dot_f32(alpha, cross, ((0,), (0,)))
    squared = dot_f32(alpha, dot_f32(gram_image, alpha, ((1,), (0,))), ((0,), (0,)))
    new_norm = old_norm - across - across.T + squared
    beta = dot_f32(norm_inverse, new_norm, ((1,), (0,)))
    direction = dir_ref[...]
    new_sol_ref[...] = sol_ref[...] + dot_f32(alpha, direction, ((0,), (0,)))
    new_res = res_ref[...] - dot_f32(alpha, image_ref[...], ((0,), (0,)))
    new_res_ref[...] = new_res
    new_dir_ref[...] = new_res + dot_f32(beta, direction, ((0,), (0,)))


VMEM_LIMIT = 48 * 1024 * 1024


def per_device(chips, points, noise_var, district, solution, residual, direction):
    rhs, count = direction.shape
    whole_count = count * chips * 2
    group = ("row", "pair")
    swap = [(0, 1), (1, 0)]
    params = pltpu.CompilerParams(vmem_limit_bytes=VMEM_LIMIT)
    packed, own, norm = pack(chips, points, district, direction, residual)
    near = lax.all_to_all(packed, group, 0, 0)
    far = lax.ppermute(near, "side", swap)
    where = lax.axis_index(group).astype(jnp.int32).reshape(1)
    dist_row = district.reshape(1, count)
    noise_row = noise_var.reshape(1, count)
    own_scratch = [pltpu.VMEM((count, LANES), F32), pltpu.VMEM((count, LANES), F32)]
    vmem = pl.BlockSpec(memory_space=pltpu.VMEM)
    product, sums = pl.pallas_call(
        first_kernel,
        out_shape=(
            jax.ShapeDtypeStruct((rhs, count), F32),
            jax.ShapeDtypeStruct((rhs + 8, count), F32),
        ),
        in_specs=[pl.BlockSpec(memory_space=pltpu.SMEM)] + [vmem] * 4,
        out_specs=(vmem, vmem),
        scratch_shapes=own_scratch,
        compiler_params=params,
        name="near_half",
    )(where, points, dist_row, own, near)
    image, gram = pl.pallas_call(
        functools.partial(second_kernel, whole_count),
        out_shape=(
            jax.ShapeDtypeStruct((rhs, count), F32),
            jax.ShapeDtypeStruct((rhs, LANES), F32),
        ),
        in_specs=[vmem] * 9,
        out_specs=(vmem, vmem),
        scratch_shapes=own_scratch,
        compiler_params=params,
        name="far_half",
    )(points, dist_row, noise_row, direction, residual, norm, product, sums, far)
    chip_gram = gram + lax.ppermute(gram, "side", swap)
    grams = lax.all_to_all(jnp.broadcast_to(chip_gram[None], (chips, rhs, LANES)), group, 0, 0)
    return pl.pallas_call(
        final_kernel,
        out_shape=tuple(jax.ShapeDtypeStruct((rhs, count), F32) for _ in range(3)),
        in_specs=[vmem] * 5,
        out_specs=(vmem,) * 3,
        compiler_params=params,
        name="final",
    )(grams, solution, residual, direction, image)


def solution(mesh):
    rows, cols = mesh.shape["row"], mesh.shape["col"]
    paired = Mesh(mesh.devices.reshape(rows, cols // 2, 2), ("row", "pair", "side"))
    samples = ("row", "pair", "side")
    wide, flat = P(None, samples), P(samples)
    return jax.shard_map(
        functools.partial(per_device, rows * cols // 2),
        mesh=paired,
        in_specs=(wide, flat, flat, wide, wide, wide),
        out_specs=(wide, wide, wide),
        check_vma=False,
    )
```

time: 225 us -> 52.3 us (0.23)
  blocking collectives: 200 us -> 32.7 us
  Pallas kernels: 0 us -> 15.6 us
  other arithmetic: 14.3 us -> 0.01 us
  matrix products: 8.77 us -> 0 us
    psum x3 -> x0, blocking collectives: 118 us -> none  [the longest x1 42.7 us: per_device(): old_norm = lax.psum(local_norm, ('row', 'col'))]
    all_gather x2 -> x0, blocking collectives: 81.5 us -> none  [the longest x1 43.5 us: per_device(): left_points = lax.all_gather(points, ('row', 'col'), axis=1, tiled=True)]
    all_to_all x0 -> x2, blocking collectives: none -> 32.7 us  [the longest x1 19.1 us: per_device(): near = lax.all_to_all(packed, group, 0, 0)]
    pallas_call x0 -> x4, Pallas kernels: none -> 15.6 us  [the longest x1 4.68 us: per_device(): pl.pallas_call(functools.partial(second_kernel, whole_count), out_shape=(...]
    another operation x10 -> x0, other arithmetic: 13.4 us -> none  [the longest x6 7.2 us: chol_solve(): factor = jnp.linalg.cholesky(matrix)]
    dot_general x9 -> x0, matrix products: 8.06 us -> none  [the longest x1 5.2 us: one_step(): jnp.dot(part_dir, matern_tile(part_points, points), preferred_element_typ...]
  transfers between devices with their start and end apart: 0 -> 2, of which waited for: 0 -> 1; matrix products, arithmetic and copies ran while one was open for 0% -> 0% of each run, Pallas kernels for 0% -> 9%
where the time goes in v1:
time: 52.3 us; the launch traced here: 51.9 us
  blocking collectives  32.7 us (63%)
  Pallas kernels  15.6 us (30%)
  local copies, waits for them, and re-layouts  1.38 us (3%)
  waiting for transfers between devices  0.84 us (2%)
  between operations  0.71 us (1%)
  starting transfers between devices  0.57 us (1%)
    all_to_all x1, blocking collectives, per_device(): near = lax.all_to_all(packed, group, 0, 0)  19.1 us
    all_to_all x1, blocking collectives, per_device(): lax.all_to_all(jnp.broadcast_to(chip_gram[None], (chips, rhs, LANES)), gr...  13.6 us
    pallas_call x1, Pallas kernels, per_device(): pl.pallas_call(functools.partial(second_kernel, whole_count), out_shape=(...  4.68 us
    pallas_call x1, Pallas kernels, per_device(): pl.pallas_call(first_kernel, out_shape=(jax.ShapeDtypeStruct((rhs, count)...  4.44 us
    pallas_call x1, Pallas kernels, per_device(): pl.pallas_call(final_kernel, out_shape=tuple((jax.ShapeDtypeStruct((rhs,...  4.44 us
    pallas_call x1, Pallas kernels, pack(): pl.pallas_call(functools.partial(pack_kernel, copies), out_shape=(jax.Sha...  2.07 us
    unnamed x16, local copies, waits for them, and re-layouts  1.36 us
  transfers between devices with their start and end apart: 2, of which 1 were waited for; matrix products, arithmetic and copies ran while one was open for 0% of the time, Pallas kernels for 9%

profile of v1, /device:TPU:0, one launch (start us, length us, event | category | flops | bytes accessed | tf_op | source)
XLA Modules:
  0.0 51.9 jit_solution(7817579621808908231)
XLA Ops:
  0.6 2.1 %pack.1 = (bf16[16,72,128]{2,1,0:T(8,128)(2,1)}, f32[40,256]{1,0:T(8,128)}, f32[32,32]{1,0:T(8,128)}) custom-call(bf16[2,256]{1,0:T(2,128)(2,1)} %points_ref.5, s32[1,256]{1,0:T(1,128)} %bitcast.3, f32[32,256]{1,0:T(8,128)} %dir_ref.5, f32[32,256]{1,0:T(8,128)} %res_ref.5), custom_call_target="tpu_custom_call" | custom-call | tf_op jit(solution)/shard_map/pack/pallas_call | solution.py:88
  2.7 0.0 copy-start.2
  2.7 19.1 %all_to_all.10.all_ref = bf16[16,72,128]{2,1,0:T(8,128)(2,1)S(1)} all-to-all(bf16[16,72,128]{2,1,0:T(8,128)(2,1)} %get-tuple-element.12), channel_id=1, replica_groups=mesh['row'=4,'pair'=4,'side'=2] {'row','pair'}, dimensions={0} | all-to-all | bytes 589824 | tf_op jit(solution)/shard_map/all_to_all | solution.py:212
  21.8 0.0 collective-permute-start
  21.8 0.0 copy-start.6
  21.8 0.0 copy-start.5
  21.8 0.0 copy-done.2
  21.8 0.7 %copy-done.6 = s32[256]{0:T(256)S(1)} copy-done((s32[256]{0:T(256)S(1)}, s32[256]{0:T(256)}, u32[]{:S(2)}) %copy-start.6) | copy-done | bytes 1048
  22.5 0.0 copy-done.5
  22.5 0.0 copy-start
  22.5 0.0 copy-start.1
  22.5 0.0 copy-start.4
  22.5 4.4 %near_half.1 = (f32[32,256]{1,0:T(8,128)S(1)}, f32[40,256]{1,0:T(8,128)S(1)}) custom-call(s32[1]{0:T(128)} %bitcast.2.where_ref, bf16[2,256]{1,0:T(2,128)(2,1)S(1)} %copy-done.5, s32[1,256]{1,0:T(1,128)S(1)} %bitcast.4, f32[40,256]{1,0:T(8,128)S(1)} %copy-done.2, bf16[16,72,128]{2,1,0:T(8,128)(2,1)S(1)} %all_to_all.10.all_ref), custom_call_target="tpu_custom_call" | custom-call | tf_op jit(solution)/shard_map/near_half/pallas_call | solution.py:219
  27.0 0.0 collective-permute-done.all_ref
  27.0 0.0 copy-start.7
  27.0 0.0 copy-done
  27.0 0.0 copy-done.1
  27.0 0.0 copy-done.4
  27.0 0.6 %copy-done.7 = f32[256]{0:T(256)S(1)} copy-done((f32[256]{0:T(256)S(1)}, f32[256]{0:T(256)}, u32[]{:S(2)}) %copy-start.7) | copy-done | bytes 1048
  27.7 4.7 %far_half.1 = (f32[32,256]{1,0:T(8,128)S(1)}, f32[32,128]{1,0:T(8,128)S(1)}) custom-call(bf16[2,256]{1,0:T(2,128)(2,1)S(1)} %copy-done.5, s32[1,256]{1,0:T(1,128)S(1)} %bitcast.5, f32[1,256]{1,0:T(1,128)S(1)} %bitcast.6, f32[32,256]{1,0:T(8,128)S(1)} %copy-done, f32[32,256]{1,0:T(8,128)S(1)} %copy-done.1, f32[32,32]{1,0:T(8,128)S(1)} %copy-done.4, ...), custom_call_target="tpu_custom_call" | custom-call | tf_op jit(solution)/shard_map/far_half/pallas_call | solution.py:231
  32.4 0.6 %collective-permute-start.1 = (f32[32,128]{1,0:T(8,128)S(1)}, f32[32,128]{1,0:T(8,128)S(1)}, u32[]{:S(2)}, u32[]{:S(2)}) collective-permute-start(f32[32,128]{1,0:T(8,128)S(1)} %get-tuple-element.15), channel_id=1, source_target_pairs={{0,1},{1,0},{2,3},{3,2},{4,5},{5,4},{6,7},{7,6},{8,9},{9,8},{10,11... | collective-permute-start | bytes 49160 | tf_op jit(solution)/shard_map/ppermute | solution.py:243
  32.9 0.8 %collective-permute-done.1 = f32[32,128]{1,0:T(8,128)S(1)} collective-permute-done((f32[32,128]{1,0:T(8,128)S(1)}, f32[32,128]{1,0:T(8,128)S(1)}, u32[]{:S(2)}, u32[]{:S(2)}) %collective-permute-start.1) | collective-permute-done | bytes 16416 | tf_op jit(solution)/shard_map/ppermute | solution.py:243
  33.8 0.0 copy-start.3
  33.8 13.6 %all_to_all.11.gram_ref = f32[16,32,128]{2,1,0:T(8,128)S(1)} all-to-all(f32[16,32,128]{2,1,0:T(8,128)S(1)} %broadcast_in_dim.2), channel_id=1, replica_groups=mesh['row'=4,'pair'=4,'side'=2] {'row','pair'}, dimensions={0} | all-to-all | bytes 524288 | tf_op jit(solution)/shard_map/all_to_all | solution.py:244
  47.4 0.0 copy-done.3
  47.4 4.4 %final.1 = (f32[32,256]{1,0:T(8,128)}, f32[32,256]{1,0:T(8,128)}, f32[32,256]{1,0:T(8,128)}) custom-call(f32[16,32,128]{2,1,0:T(8,128)S(1)} %all_to_all.11.gram_ref, f32[32,256]{1,0:T(8,128)S(1)} %copy-done.3, f32[32,256]{1,0:T(8,128)S(1)} %copy-done.1, f32[32,256]{1,0:T(8,128)S(1)} %copy-done, f32[32,256]{1,0:T(8,128)S(1)} %get-tuple-element.16.image_ref), custom_call_target="tpu_custom_call" | custom-call | tf_op jit(solution)/shard_map/final/pallas_call | solution.py:245
  (2 shorter events, 0.0 us)
Async XLA Ops:
  2.7 19.1 %copy-start.2 = (f32[40,256]{1,0:T(8,128)S(1)}, f32[40,256]{1,0:T(8,128)}, u32[]{:S(2)}) copy-start(f32[40,256]{1,0:T(8,128)} %get-tuple-element.11.own_ref) | copy-start | bytes 122884
  21.8 5.2 %collective-permute-start = (bf16[16,72,128]{2,1,0:T(8,128)(2,1)S(1)}, bf16[16,72,128]{2,1,0:T(8,128)(2,1)S(1)}, u32[]{:S(2)}, u32[]{:S(2)}) collective-permute-start(bf16[16,72,128]{2,1,0:T(8,128)(2,1)S(1)} %all_to_all.10.all_ref), channel_id=1, source_target_pairs={{0,1},{1,0},{2,3},{3,2},{4,5},{5,4},{6,7},{7,6},{8,9},{9,8},{10,11... | collective-permute-start | bytes 884744 | tf_op jit(solution)/shard_map/ppermute | solution.py:213
  21.8 0.7 %copy-start.6 = (s32[256]{0:T(256)S(1)}, s32[256]{0:T(256)}, u32[]{:S(2)}) copy-start(s32[256]{0:T(256)} %param.8) | copy-start | bytes 3076
  21.8 0.7 %copy-start.5 = (bf16[2,256]{1,0:T(2,128)(2,1)S(1)}, bf16[2,256]{1,0:T(2,128)(2,1)}, u32[]{:S(2)}) copy-start(bf16[2,256]{1,0:T(2,128)(2,1)} %points_ref.5) | copy-start | bytes 3076
  22.5 4.5 %copy-start = (f32[32,256]{1,0:T(8,128)S(1)}, f32[32,256]{1,0:T(8,128)}, u32[]{:S(2)}) copy-start(f32[32,256]{1,0:T(8,128)} %dir_ref.5) | copy-start | bytes 98308
  22.5 4.5 %copy-start.1 = (f32[32,256]{1,0:T(8,128)S(1)}, f32[32,256]{1,0:T(8,128)}, u32[]{:S(2)}) copy-start(f32[32,256]{1,0:T(8,128)} %res_ref.5) | copy-start | bytes 98308
  22.5 4.5 %copy-start.4 = (f32[32,32]{1,0:T(8,128)S(1)}, f32[32,32]{1,0:T(8,128)}, u32[]{:S(2)}) copy-start(f32[32,32]{1,0:T(8,128)} %get-tuple-element.10.norm_ref) | copy-start | bytes 12292
  27.0 0.7 %copy-start.7 = (f32[256]{0:T(256)S(1)}, f32[256]{0:T(256)}, u32[]{:S(2)}) copy-start(f32[256]{0:T(256)} %param.7) | copy-start | bytes 3076
  32.4 1.4 %collective-permute-start.1 = (f32[32,128]{1,0:T(8,128)S(1)}, f32[32,128]{1,0:T(8,128)S(1)}, u32[]{:S(2)}, u32[]{:S(2)}) collective-permute-start(f32[32,128]{1,0:T(8,128)S(1)} %get-tuple-element.15), channel_id=1, source_target_pairs={{0,1},{1,0},{2,3},{3,2},{4,5},{5,4},{6,7},{7,6},{8,9},{9,8},{10,11... | collective-permute-start | bytes 49160 | tf_op jit(solution)/shard_map/ppermute | solution.py:243
  33.8 13.6 %copy-start.3 = (f32[32,256]{1,0:T(8,128)S(1)}, f32[32,256]{1,0:T(8,128)}, u32[]{:S(2)}) copy-start(f32[32,256]{1,0:T(8,128)} %sol_ref.1) | copy-start | bytes 98308

commit v2 on v1

v2 whole, which is shorter than its diff:
```python
import functools
import math

import jax
import jax.numpy as jnp
from jax import lax
from jax.experimental import pallas as pl
from jax.experimental.pallas import tpu as pltpu
from jax.sharding import Mesh, PartitionSpec as P

root_three = math.sqrt(3.0)
corr_range = 0.05
district_gain = 0.5
LANES = 128
ROWS = 72
F32, BF16 = jnp.float32, jnp.bfloat16


def dot_f32(left, right, dims):
    return lax.dot_general(
        left, right, (dims, ((), ())), precision=lax.Precision.HIGHEST, preferred_element_type=F32
    )


def dot_bf16(left, right, dims):
    return lax.dot_general(left, right, (dims, ((), ())), preferred_element_type=F32)


def three_pieces(vals):
    high = vals.astype(BF16)
    rest = vals - high.astype(F32)
    mid = rest.astype(BF16)
    low = (rest - mid.astype(F32)).astype(BF16)
    return high, mid, low


def pack_kernel(points_ref, dist_ref, noise_ref, dir_ref, pack_ref, own_ref):
    rhs, count = dir_ref.shape
    direction = dir_ref[...]
    dist = dist_ref[...]
    high, mid, low = three_pieces(direction)
    ones = jnp.ones((LANES - 3 * rhs, count), BF16)
    stacked = jnp.concatenate([high, mid, low, ones], axis=0)
    labels = lax.broadcasted_iota(jnp.int32, (64, count), 0)
    onehot = (labels == dist).astype(F32).astype(BF16)
    same = dot_bf16(onehot, onehot, ((0,), (0,))).astype(BF16)
    sums = dot_bf16(stacked, same, ((1,), (0,)))
    pts = points_ref[...].astype(F32)
    own_ref[0:rhs, :] = sums[0:rhs] + sums[rhs : 2 * rhs] + sums[2 * rhs : 3 * rhs]
    own_ref[rhs:, :] = sums[3 * rhs : 3 * rhs + 8]
    own_ref[rhs + 1 : rhs + 2, :] = dist.astype(F32)
    own_ref[rhs + 2 : rhs + 3, :] = noise_ref[...]
    own_ref[rhs + 3 : rhs + 5, :] = pts
    first = dist[:, 0:1]
    last = dist[:, count - 1 : count]
    row = lax.broadcasted_iota(jnp.int32, (8, count), 0)
    picked = jnp.where(row == 0, first, last)
    wanted = (row == 0) | ((row == 1) & (first != last))
    mask = (wanted & (dist == picked)).astype(F32).astype(BF16)
    edge = dot_bf16(mask, stacked, ((1,), (1,)))
    total = edge + pltpu.roll(edge, LANES - rhs, 1) + pltpu.roll(edge, LANES - 2 * rhs, 1)
    lane = lax.broadcasted_iota(jnp.int32, (8, LANES), 1)
    total = jnp.where(lane < rhs, total, 0.0)
    e_high, e_mid, e_low = three_pieces(total)
    row8 = lax.broadcasted_iota(jnp.int32, (8, LANES), 0)
    label = jnp.where(row8 == 0, first, last).astype(F32)
    extras = (
        e_high.astype(F32)
        + pltpu.roll(e_mid.astype(F32), rhs, 1)
        + pltpu.roll(e_low.astype(F32), 2 * rhs, 1)
    )
    extras = jnp.where(lane == 3 * rhs, label, extras)
    extras = jnp.where(lane == 3 * rhs + 1, edge, extras)
    tail = jnp.concatenate(
        [pts[:, 0:LANES], pts[:, LANES:], extras[0:2, :], jnp.zeros((2, LANES), F32)], axis=0
    )
    pack_ref[0:rhs, :] = high[:, 0:LANES]
    pack_ref[rhs : 2 * rhs, :] = high[:, LANES:]
    pack_ref[2 * rhs :, :] = tail.astype(BF16)


def half_product(skip, own_ref, all_ref, own_x, own_y):
    blocks = all_ref.shape[0]
    count = own_ref.shape[1]
    rhs = 32
    scale = root_three / corr_range
    own = own_ref[rhs:, :]
    pts = own.astype(BF16)
    row = lax.broadcasted_iota(jnp.int32, (8, LANES), 0)
    own_x[...] = dot_bf16(pts, (row == 3).astype(F32).astype(BF16), ((0,), (0,))) * scale
    own_y[...] = dot_bf16(pts, (row == 4).astype(F32).astype(BF16), ((0,), (0,))) * scale
    step = 16
    to_two = -math.log2(math.e)

    def one_block(index, acc):
        block = all_ref[index]
        tail = block[2 * rhs :, :].astype(F32) * scale
        halves = []
        for half in range(2):
            right_x = tail[2 * half : 2 * half + 1, :]
            right_y = tail[2 * half + 1 : 2 * half + 2, :]
            parts = []
            for start in range(0, count, step):
                dx = own_x[start : start + step, :] - right_x
                dy = own_y[start : start + step, :] - right_y
                square = jnp.maximum(dx * dx + dy * dy, 1e-30)
                scaled = square * lax.rsqrt(square)
                parts.append(((1.0 + scaled) * jnp.exp2(scaled * to_two)).astype(BF16))
            halves.append(jnp.concatenate(parts, axis=0))
        tile = jnp.concatenate(halves, axis=1)
        left = jnp.concatenate([block[0:rhs, :], block[rhs : 2 * rhs, :]], axis=1)
        return acc + dot_bf16(left, tile, ((1,), (1,)))

    def some_blocks(index, acc):
        for inner in range(batch):
            acc = one_block(index * batch + inner, acc)
        return acc

    batch = math.gcd(blocks, 16)
    product = jnp.zeros((rhs, count), F32)
    if blocks == batch:
        product = some_blocks(0, product)
    else:
        product = lax.fori_loop(0, blocks // batch, some_blocks, product)

    edges = all_ref[:, 2 * rhs :, :].astype(F32).reshape(blocks * 8, LANES)
    place = lax.broadcasted_iota(jnp.int32, (blocks * 8, count), 0)
    kind = place % 8
    good = ((kind == 4) | (kind == 5)) & (place // 8 != skip)
    match = good & (edges[:, 3 * rhs : 3 * rhs + 1] == own[1:2, :])
    sums = dot_bf16(edges.astype(BF16), match.astype(F32).astype(BF16), ((0,), (0,)))
    extra = sums[0:rhs] + sums[rhs : 2 * rhs] + sums[2 * rhs : 3 * rhs]
    return product, extra, sums[3 * rhs + 1 : 3 * rhs + 2]


def first_kernel(where_ref, own_ref, res_ref, all_ref, product_ref, sums_ref, norm_ref, own_x, own_y):
    product, extra, number = half_product(where_ref[0], own_ref, all_ref, own_x, own_y)
    product_ref[...] = product
    sums_ref[0:32, :] = own_ref[0:32, :] + extra
    sums_ref[32:40, :] = own_ref[32:40, :]
    sums_ref[32:33, :] = own_ref[32:33, :] + number
    norm_ref[...] = dot_f32(res_ref[...], res_ref[...], ((1,), (1,)))


def second_kernel(
    whole_count, dir_ref, res_ref, norm_ref, product_ref, sums_ref, all_ref, image_ref, gram_ref, own_x, own_y
):
    product, extra, number = half_product(-1, sums_ref, all_ref, own_x, own_y)
    product = product + product_ref[...]
    size = sums_ref[32:33, :] + number
    district_part = (sums_ref[0:32, :] + extra) / jnp.sqrt(size)
    direction = dir_ref[...]
    kernel_scale = 1.0 / (corr_range * math.sqrt(whole_count))
    image = sums_ref[34:35, :] * direction + product * kernel_scale + district_gain * district_part
    image_ref[...] = image
    right = jnp.concatenate([direction, res_ref[...], image], axis=0)
    gram_ref[:, 0:96] = dot_f32(image, right, ((1,), (1,)))
    gram_ref[:, 96:128] = norm_ref[...]


def eliminate(work, step):
    rows = lax.broadcasted_iota(jnp.int32, work.shape, 0)
    one, two = work[:, step : step + 1], work[:, step + 1 : step + 2]
    one, two = jnp.broadcast_to(one, work.shape), jnp.broadcast_to(two, work.shape)
    row_one, row_two = work[step : step + 1, :], work[step + 1 : step + 2, :]
    p11, p12 = one[step : step + 1, :], two[step : step + 1, :]
    p21, p22 = one[step + 1 : step + 2, :], two[step + 1 : step + 2, :]
    inverse = 1.0 / (p11 * p22 - p12 * p21)
    new_one = (p22 * row_one - p12 * row_two) * inverse
    new_two = (p11 * row_two - p21 * row_one) * inverse
    rest = work - one * new_one - two * new_two
    return jnp.where(rows == step, new_one, jnp.where(rows == step + 1, new_two, rest))


def final_kernel(gram_ref, sol_ref, res_ref, dir_ref, image_ref, new_sol_ref, new_res_ref, new_dir_ref):
    rhs = 32
    total = gram_ref[0]
    for n in range(1, gram_ref.shape[0]):
        total = total + gram_ref[n]
    curv = total[:, 0:32]
    cross = total[:, 32:64]
    gram_image = total[:, 64:96]
    old_norm = total[:, 96:128]
    curv = 0.5 * (curv + curv.T)
    first = jnp.concatenate([curv, old_norm, cross, gram_image], axis=1)
    second = jnp.concatenate([old_norm, cross.T, jnp.zeros((rhs, 64), F32)], axis=1)
    for step in range(0, rhs, 2):
        first = eliminate(first, step)
        second = eliminate(second, step)
    alpha = first[:, 32:64]
    row = lax.broadcasted_iota(jnp.int32, (rhs, rhs), 0)
    col = lax.broadcasted_iota(jnp.int32, (rhs, rhs), 1)
    eye = (row == col).astype(F32)
    beta = eye - first[:, 64:96] + dot_f32(first[:, 96:128] - second[:, 32:64], alpha, ((1,), (0,)))
    direction = dir_ref[...]
    new_sol_ref[...] = sol_ref[...] + dot_f32(alpha, direction, ((0,), (0,)))
    new_res = res_ref[...] - dot_f32(alpha, image_ref[...], ((0,), (0,)))
    new_res_ref[...] = new_res
    new_dir_ref[...] = new_res + dot_f32(beta, direction, ((0,), (0,)))


VMEM_LIMIT = 48 * 1024 * 1024


def per_device(chips, points, noise_var, district, solution, residual, direction):
    rhs, count = direction.shape
    whole_count = count * chips * 2
    group = ("row", "pair")
    swap = [(0, 1), (1, 0)]
    params = pltpu.CompilerParams(vmem_limit_bytes=VMEM_LIMIT)
    wide = jax.ShapeDtypeStruct((rhs, count), F32)
    own_shape = jax.ShapeDtypeStruct((rhs + 8, count), F32)
    vmem = pl.BlockSpec(memory_space=pltpu.VMEM)
    block, own = pl.pallas_call(
        pack_kernel,
        out_shape=(jax.ShapeDtypeStruct((ROWS, LANES), BF16), own_shape),
        name="pack",
    )(points, district.reshape(1, count), noise_var.reshape(1, count), direction)
    near = lax.all_to_all(jnp.broadcast_to(block[None], (chips, ROWS, LANES)), group, 0, 0)
    far = lax.ppermute(near, "side", swap)
    where = lax.axis_index(group).astype(jnp.int32).reshape(1)
    own_scratch = [pltpu.VMEM((count, LANES), F32), pltpu.VMEM((count, LANES), F32)]
    product, sums, norm = pl.pallas_call(
        first_kernel,
        out_shape=(wide, own_shape, jax.ShapeDtypeStruct((rhs, rhs), F32)),
        in_specs=[pl.BlockSpec(memory_space=pltpu.SMEM)] + [vmem] * 3,
        out_specs=(vmem,) * 3,
        scratch_shapes=own_scratch,
        compiler_params=params,
        name="near_half",
    )(where, own, residual, near)
    image, gram = pl.pallas_call(
        functools.partial(second_kernel, whole_count),
        out_shape=(wide, jax.ShapeDtypeStruct((rhs, LANES), F32)),
        in_specs=[vmem] * 6,
        out_specs=(vmem, vmem),
        scratch_shapes=own_scratch,
        compiler_params=params,
        name="far_half",
    )(direction, residual, norm, product, sums, far)
    chip_gram = gram + lax.ppermute(gram, "side", swap)
    grams = lax.all_to_all(jnp.broadcast_to(chip_gram[None], (chips, rhs, LANES)), group, 0, 0)
    return pl.pallas_call(
        final_kernel,
        out_shape=(wide,) * 3,
        in_specs=[vmem] * 5,
        out_specs=(vmem,) * 3,
        compiler_params=params,
        name="final",
    )(grams, solution, residual, direction, image)


def solution(mesh):
    rows, cols = mesh.shape["row"], mesh.shape["col"]
    paired = Mesh(mesh.devices.reshape(rows, cols // 2, 2), ("row", "pair", "side"))
    samples = ("row", "pair", "side")
    wide, flat = P(None, samples), P(samples)
    return jax.shard_map(
        functools.partial(per_device, rows * cols // 2),
        mesh=paired,
        in_specs=(wide, flat, flat, wide, wide, wide),
        out_specs=(wide, wide, wide),
        check_vma=False,
    )
```

time: 52.3 us -> 45.7 us (0.87)
  Pallas kernels: 15.6 us -> 9.84 us
  local copies, waits for them, and re-layouts: 1.38 us -> 0.8 us
    pallas_call x3, Pallas kernels: 11 us -> 7.24 us  [the longest x1 2.91 us: per_device(): pl.pallas_call(final_kernel, out_shape=(wide,) * 3, in_specs=[vmem] * 5,...]
    pallas_call x1, Pallas kernels: 4.68 us -> 2.6 us  [per_device(): pl.pallas_call(functools.partial(second_kernel, whole_count), out_shape=(...]
    unnamed x16 -> x8, local copies, waits for them, and re-layouts: 1.36 us -> 0.02 us
    broadcast_in_dim x0 -> x1, local copies, waits for them, and re-layouts: none -> 0.76 us  [per_device(): jnp.broadcast_to(block[None], (chips, ROWS, LANES))]
  transfers between devices with their start and end apart: 2 -> 2, of which waited for: 1 -> 1; matrix products, arithmetic and copies ran while one was open for 0% -> 0% of each run, Pallas kernels for 9% -> 5%
where the time goes in v2:
time: 45.7 us; the launch traced here: 45.2 us
  blocking collectives  32.5 us (71%)
  Pallas kernels  9.84 us (22%)
  waiting for transfers between devices  0.85 us (2%)
  local copies, waits for them, and re-layouts  0.8 us (2%)
  between operations  0.7 us (2%)
  starting transfers between devices  0.51 us (1%)
    all_to_all x1, blocking collectives, per_device(): lax.all_to_all(jnp.broadcast_to(block[None], (chips, ROWS, LANES)), group...  18.9 us
    all_to_all x1, blocking collectives, per_device(): lax.all_to_all(jnp.broadcast_to(chip_gram[None], (chips, rhs, LANES)), gr...  13.6 us
    pallas_call x1, Pallas kernels, per_device(): pl.pallas_call(final_kernel, out_shape=(wide,) * 3, in_specs=[vmem] * 5,...  2.91 us
    pallas_call x1, Pallas kernels, per_device(): pl.pallas_call(functools.partial(second_kernel, whole_count), out_shape=(...  2.6 us
    pallas_call x1, Pallas kernels, per_device(): pl.pallas_call(first_kernel, out_shape=(wide, own_shape, jax.ShapeDtypeSt...  2.36 us
    pallas_call x1, Pallas kernels, per_device(): pl.pallas_call(pack_kernel, out_shape=(jax.ShapeDtypeStruct((ROWS, LANES)...  1.96 us
  transfers between devices with their start and end apart: 2, of which 1 were waited for; matrix products, arithmetic and copies ran while one was open for 0% of the time, Pallas kernels for 5%

profile of v2, /device:TPU:0, one launch (start us, length us, event | category | flops | bytes accessed | tf_op | source)
XLA Modules:
  0.0 45.2 jit_solution(5400302154828400839)
XLA Ops:
  0.6 2.0 %pack.1 = (bf16[72,128]{1,0:T(8,128)(2,1)}, f32[40,256]{1,0:T(8,128)}) custom-call(bf16[2,256]{1,0:T(2,128)(2,1)} %points_ref.1, s32[1,256]{1,0:T(1,128)} %bitcast.3, f32[1,256]{1,0:T(1,128)} %bitcast.4, f32[32,256]{1,0:T(8,128)} %dir_ref.5), custom_call_target="tpu_custom_call" | custom-call | tf_op jit(solution)/shard_map/pack/pallas_call | solution.py:214
  2.6 0.8 %broadcast_in_dim.4 = bf16[16,72,128]{2,1,0:T(8,128)(2,1)S(1)} broadcast(bf16[72,128]{1,0:T(8,128)(2,1)} %get-tuple-element.11), dimensions={1,2} | broadcast | bytes 313344 | tf_op jit(solution)/shard_map/broadcast_in_dim | solution.py:219
  3.4 0.0 copy-start
  3.4 0.0 copy-start.2
  3.4 18.9 %all_to_all.10.all_ref = bf16[16,72,128]{2,1,0:T(8,128)(2,1)S(1)} all-to-all(bf16[16,72,128]{2,1,0:T(8,128)(2,1)S(1)} %broadcast_in_dim.4), channel_id=1, replica_groups=mesh['row'=4,'pair'=4,'side'=2] {'row','pair'}, dimensions={0} | all-to-all | bytes 589824 | tf_op jit(solution)/shard_map/all_to_all | solution.py:219
  22.3 0.0 collective-permute-start
  22.3 0.0 copy-done
  22.3 0.0 copy-done.2
  22.3 0.0 copy-start.1
  22.3 2.4 %near_half.1 = (f32[32,256]{1,0:T(8,128)S(1)}, f32[40,256]{1,0:T(8,128)S(1)}, f32[32,32]{1,0:T(8,128)S(1)}) custom-call(s32[1]{0:T(128)} %bitcast.where_ref, f32[40,256]{1,0:T(8,128)S(1)} %copy-done.2, f32[32,256]{1,0:T(8,128)S(1)} %copy-done, bf16[16,72,128]{2,1,0:T(8,128)(2,1)S(1)} %all_to_all.10.all_ref), custom_call_target="tpu_custom_call" | custom-call | tf_op jit(solution)/shard_map/near_half/pallas_call | solution.py:223
  24.7 0.0 collective-permute-done.all_ref
  24.7 0.0 copy-done.1
  24.7 2.6 %far_half.1 = (f32[32,256]{1,0:T(8,128)S(1)}, f32[32,128]{1,0:T(8,128)S(1)}) custom-call(f32[32,256]{1,0:T(8,128)S(1)} %copy-done.1, f32[32,256]{1,0:T(8,128)S(1)} %copy-done, f32[32,32]{1,0:T(8,128)S(1)} %get-tuple-element.12.norm_ref, f32[32,256]{1,0:T(8,128)S(1)} %get-tuple-element.13.product_ref, f32[40,256]{1,0:T(8,128)S(1)} %get-tuple-element.14.sums_ref, ...), custom_call_target="tpu_custom_call" | custom-call | tf_op jit(solution)/shard_map/far_half/pallas_call | solution.py:232
  27.3 0.5 %collective-permute-start.1 = (f32[32,128]{1,0:T(8,128)S(1)}, f32[32,128]{1,0:T(8,128)S(1)}, u32[]{:S(2)}, u32[]{:S(2)}) collective-permute-start(f32[32,128]{1,0:T(8,128)S(1)} %get-tuple-element.15), channel_id=1, source_target_pairs={{0,1},{1,0},{2,3},{3,2},{4,5},{5,4},{6,7},{7,6},{8,9},{9,8},{10,11... | collective-permute-start | bytes 49160 | tf_op jit(solution)/shard_map/ppermute | solution.py:241
  27.8 0.8 %collective-permute-done.1 = f32[32,128]{1,0:T(8,128)S(1)} collective-permute-done((f32[32,128]{1,0:T(8,128)S(1)}, f32[32,128]{1,0:T(8,128)S(1)}, u32[]{:S(2)}, u32[]{:S(2)}) %collective-permute-start.1) | collective-permute-done | bytes 16416 | tf_op jit(solution)/shard_map/ppermute | solution.py:241
  28.7 0.0 copy-start.3
  28.7 13.6 %all_to_all.11.gram_ref = f32[16,32,128]{2,1,0:T(8,128)S(1)} all-to-all(f32[16,32,128]{2,1,0:T(8,128)S(1)} %broadcast_in_dim.5), channel_id=1, replica_groups=mesh['row'=4,'pair'=4,'side'=2] {'row','pair'}, dimensions={0} | all-to-all | bytes 524288 | tf_op jit(solution)/shard_map/all_to_all | solution.py:242
  42.3 0.0 copy-done.3
  42.3 2.9 %final.1 = (f32[32,256]{1,0:T(8,128)}, f32[32,256]{1,0:T(8,128)}, f32[32,256]{1,0:T(8,128)}) custom-call(f32[16,32,128]{2,1,0:T(8,128)S(1)} %all_to_all.11.gram_ref, f32[32,256]{1,0:T(8,128)S(1)} %copy-done.3, f32[32,256]{1,0:T(8,128)S(1)} %copy-done, f32[32,256]{1,0:T(8,128)S(1)} %copy-done.1, f32[32,256]{1,0:T(8,128)S(1)} %get-tuple-element.16.image_ref), custom_call_target="tpu_custom_call" | custom-call | tf_op jit(solution)/shard_map/final/pallas_call | solution.py:243
  (2 shorter events, 0.0 us)
Async XLA Ops:
  3.4 19.0 %copy-start = (f32[32,256]{1,0:T(8,128)S(1)}, f32[32,256]{1,0:T(8,128)}, u32[]{:S(2)}) copy-start(f32[32,256]{1,0:T(8,128)} %res_ref.5) | copy-start | bytes 98308
  3.4 18.9 %copy-start.2 = (f32[40,256]{1,0:T(8,128)S(1)}, f32[40,256]{1,0:T(8,128)}, u32[]{:S(2)}) copy-start(f32[40,256]{1,0:T(8,128)} %get-tuple-element.10.own_ref) | copy-start | bytes 122884
  22.3 2.4 %collective-permute-start = (bf16[16,72,128]{2,1,0:T(8,128)(2,1)S(1)}, bf16[16,72,128]{2,1,0:T(8,128)(2,1)S(1)}, u32[]{:S(2)}, u32[]{:S(2)}) collective-permute-start(bf16[16,72,128]{2,1,0:T(8,128)(2,1)S(1)} %all_to_all.10.all_ref), channel_id=1, source_target_pairs={{0,1},{1,0},{2,3},{3,2},{4,5},{5,4},{6,7},{7,6},{8,9},{9,8},{10,11... | collective-permute-start | bytes 884744 | tf_op jit(solution)/shard_map/ppermute | solution.py:220
  22.3 2.4 %copy-start.1 = (f32[32,256]{1,0:T(8,128)S(1)}, f32[32,256]{1,0:T(8,128)}, u32[]{:S(2)}) copy-start(f32[32,256]{1,0:T(8,128)} %dir_ref.5) | copy-start | bytes 98308
  27.3 1.3 %collective-permute-start.1 = (f32[32,128]{1,0:T(8,128)S(1)}, f32[32,128]{1,0:T(8,128)S(1)}, u32[]{:S(2)}, u32[]{:S(2)}) collective-permute-start(f32[32,128]{1,0:T(8,128)S(1)} %get-tuple-element.15), channel_id=1, source_target_pairs={{0,1},{1,0},{2,3},{3,2},{4,5},{5,4},{6,7},{7,6},{8,9},{9,8},{10,11... | collective-permute-start | bytes 49160 | tf_op jit(solution)/shard_map/ppermute | solution.py:241
  28.7 13.6 %copy-start.3 = (f32[32,256]{1,0:T(8,128)S(1)}, f32[32,256]{1,0:T(8,128)}, u32[]{:S(2)}) copy-start(f32[32,256]{1,0:T(8,128)} %sol_ref.1) | copy-start | bytes 98308

commit v3 on v2

v3 whole, which is shorter than its diff:
```python
import functools
import math

import jax
import jax.numpy as jnp
from jax import lax
from jax.experimental import pallas as pl
from jax.experimental.pallas import tpu as pltpu
from jax.sharding import Mesh, PartitionSpec as P

root_three = math.sqrt(3.0)
corr_range = 0.05
district_gain = 0.5
LANES = 128
ROWS = 72
F32, BF16 = jnp.float32, jnp.bfloat16


def dot_f32(left, right, dims):
    return lax.dot_general(
        left, right, (dims, ((), ())), precision=lax.Precision.HIGHEST, preferred_element_type=F32
    )


def dot_bf16(left, right, dims):
    return lax.dot_general(left, right, (dims, ((), ())), preferred_element_type=F32)


def three_pieces(vals):
    high = vals.astype(BF16)
    rest = vals - high.astype(F32)
    mid = rest.astype(BF16)
    low = (rest - mid.astype(F32)).astype(BF16)
    return high, mid, low


def stack_pieces(vals):
    rows, count = vals.shape
    ones = jnp.ones((LANES - 3 * rows, count), BF16)
    return jnp.concatenate([*three_pieces(vals), ones], axis=0)


def pack_kernel(
    points_hbm, dist_hbm, noise_hbm, dir_hbm, pack_ref, own_ref, points_ref, dist_ref, noise_ref, dir_ref, sems
):
    pairs = ((points_hbm, points_ref), (dist_hbm, dist_ref), (noise_hbm, noise_ref), (dir_hbm, dir_ref))
    copies = [pltpu.make_async_copy(src, dst, sems.at[n]) for n, (src, dst) in enumerate(pairs)]
    for copy in copies:
        copy.start()
    for copy in copies:
        copy.wait()
    rhs, count = dir_ref.shape
    dist = dist_ref[...]
    pts = points_ref[...].astype(F32)
    own_ref[...] = jnp.concatenate(
        [pts, dist.astype(F32), noise_ref[...], jnp.zeros((4, count), F32)], axis=0
    )
    stacked = stack_pieces(dir_ref[...])
    high = stacked[0:rhs]
    first = dist[:, 0:1]
    last = dist[:, count - 1 : count]
    row = lax.broadcasted_iota(jnp.int32, (8, count), 0)
    picked = jnp.where(row == 0, first, last)
    wanted = (row == 0) | ((row == 1) & (first != last))
    mask = (wanted & (dist == picked)).astype(F32).astype(BF16)
    edge = dot_bf16(mask, stacked, ((1,), (1,)))
    total = edge + pltpu.roll(edge, LANES - rhs, 1) + pltpu.roll(edge, LANES - 2 * rhs, 1)
    lane = lax.broadcasted_iota(jnp.int32, (8, LANES), 1)
    total = jnp.where(lane < rhs, total, 0.0)
    e_high, e_mid, e_low = three_pieces(total)
    row8 = lax.broadcasted_iota(jnp.int32, (8, LANES), 0)
    label = jnp.where(row8 == 0, first, last).astype(F32)
    extras = (
        e_high.astype(F32)
        + pltpu.roll(e_mid.astype(F32), rhs, 1)
        + pltpu.roll(e_low.astype(F32), 2 * rhs, 1)
    )
    extras = jnp.where(lane == 3 * rhs, label, extras)
    extras = jnp.where(lane == 3 * rhs + 1, edge, extras)
    tail = jnp.concatenate(
        [pts[:, 0:LANES], pts[:, LANES:], extras[0:2, :], jnp.zeros((2, LANES), F32)], axis=0
    )
    pack_ref[0:rhs, :] = high[:, 0:LANES]
    pack_ref[rhs : 2 * rhs, :] = high[:, LANES:]
    pack_ref[2 * rhs :, :] = tail.astype(BF16)


def own_side(own):
    scale = 3.0 / corr_range**2
    row = lax.broadcasted_iota(jnp.int32, own.shape, 0)
    cross = jnp.where(row < 2, own * (-2.0 * scale), 0.0)
    square = own * own
    norm = scale * (square[0:1] + square[1:2])
    cross_high, cross_low, _ = three_pieces(cross)
    high, mid, low = (piece.astype(F32) for piece in three_pieces(norm))
    ones = jnp.where(row < 2, scale, 0.0)
    norms = jnp.where(row == 0, high, jnp.where(row == 1, mid, jnp.where(row == 2, low, 0.0)))
    return jnp.concatenate([cross_high.astype(F32), cross_low.astype(F32), ones, ones, norms], axis=0)


def other_side(tail):
    left = tail.astype(F32)
    right = pltpu.roll(left, left.shape[0] - 2, 0)
    coords = jnp.concatenate([left, right], axis=1)
    square = coords * coords
    high = square.astype(BF16).astype(F32)
    return jnp.concatenate([coords, coords, high, square - high, jnp.ones_like(coords)], axis=0).astype(BF16)


def half_product(skip, own_ref, all_ref, side):
    blocks = all_ref.shape[0]
    count = own_ref.shape[1]
    rhs = 32
    own = own_ref[...]
    side[...] = own_side(own).T.astype(BF16)
    to_two = -math.log2(math.e)

    def one_block(index, acc):
        block = all_ref[index]
        square = dot_bf16(side[...], other_side(block[2 * rhs :, :]), ((1,), (0,)))
        square = jnp.maximum(square, 1e-30)
        scaled = square * lax.rsqrt(square)
        tile = ((1.0 + scaled) * jnp.exp2(scaled * to_two)).astype(BF16)
        left = jnp.concatenate([block[0:rhs, :], block[rhs : 2 * rhs, :]], axis=1)
        return acc + dot_bf16(left, tile, ((1,), (1,)))

    def some_blocks(index, acc):
        for inner in range(batch):
            acc = one_block(index * batch + inner, acc)
        return acc

    batch = math.gcd(blocks, 16)
    product = jnp.zeros((rhs, count), F32)
    if blocks == batch:
        product = some_blocks(0, product)
    else:
        product = lax.fori_loop(0, blocks // batch, some_blocks, product)

    edges = all_ref[:, 2 * rhs :, :].astype(F32).reshape(blocks * 8, LANES)
    place = lax.broadcasted_iota(jnp.int32, (blocks * 8, count), 0)
    kind = place % 8
    good = ((kind == 4) | (kind == 5)) & (place // 8 != skip)
    match = good & (edges[:, 3 * rhs : 3 * rhs + 1] == own[2:3, :])
    sums = dot_bf16(edges.astype(BF16), match.astype(F32).astype(BF16), ((0,), (0,)))
    extra = sums[0:rhs] + sums[rhs : 2 * rhs] + sums[2 * rhs : 3 * rhs]
    return product, extra, sums[3 * rhs + 1 : 3 * rhs + 2]


def first_kernel(own_ref, dir_ref, res_ref, all_ref, product_ref, sums_ref, norm_ref, side):
    rhs, count = dir_ref.shape
    product, extra, number = half_product(lax.axis_index(("row", "pair")), own_ref, all_ref, side)
    product_ref[...] = product
    labels = lax.broadcasted_iota(jnp.int32, (64, count), 0).astype(F32)
    onehot = (labels == own_ref[2:3, :]).astype(F32).astype(BF16)
    same = dot_bf16(onehot, onehot, ((0,), (0,))).astype(BF16)
    sums = dot_bf16(stack_pieces(dir_ref[...]), same, ((1,), (0,)))
    sums_ref[0:rhs, :] = sums[0:rhs] + sums[rhs : 2 * rhs] + sums[2 * rhs : 3 * rhs] + extra
    sums_ref[rhs:, :] = sums[3 * rhs : 3 * rhs + 8] + number
    norm_ref[...] = dot_f32(res_ref[...], res_ref[...], ((1,), (1,)))


def second_kernel(
    whole_count, own_ref, dir_ref, res_ref, norm_ref, product_ref, sums_ref, all_ref,
    image_ref, keep_ref, send_ref, side, gram,
):
    product, extra, number = half_product(-1, own_ref, all_ref, side)
    product = product + product_ref[...]
    size = sums_ref[32:33, :] + number
    district_part = (sums_ref[0:32, :] + extra) / jnp.sqrt(size)
    direction = dir_ref[...]
    kernel_scale = 1.0 / (corr_range * math.sqrt(whole_count))
    image = own_ref[3:4, :] * direction + product * kernel_scale + district_gain * district_part
    image_ref[...] = image
    right = jnp.concatenate([direction, res_ref[...], image], axis=0)
    gram[:, 0:96] = dot_f32(image, right, ((1,), (1,)))
    gram[:, 96:128] = norm_ref[...]
    half = keep_ref.shape[0]
    core = lax.axis_index("side")
    keep_ref[...] = gram[pl.ds(pl.multiple_of(core * half, half), half), :]
    send_ref[...] = gram[pl.ds(pl.multiple_of((1 - core) * half, half), half), :]


def eliminate(work, step):
    rows = lax.broadcasted_iota(jnp.int32, work.shape, 0)
    cols = [jnp.broadcast_to(work[:, step + n : step + n + 1], work.shape) for n in range(4)]
    line = [work[step + n : step + n + 1, :] for n in range(4)]
    piv = [[cols[m][step + n : step + n + 1, :] for m in range(4)] for n in range(4)]
    inverse = 1.0 / (piv[0][0] * piv[1][1] - piv[0][1] * piv[1][0])

    def first_block(top, bottom):
        return (piv[1][1] * top - piv[0][1] * bottom) * inverse, (piv[0][0] * bottom - piv[1][0] * top) * inverse

    new0, new1 = first_block(line[0], line[1])
    cross = [first_block(piv[0][m], piv[1][m]) for m in (2, 3)]
    rest = [[piv[n][m + 2] - piv[n][0] * cross[m][0] - piv[n][1] * cross[m][1] for m in range(2)] for n in (2, 3)]
    inverse_rest = 1.0 / (rest[0][0] * rest[1][1] - rest[0][1] * rest[1][0])
    left2 = line[2] - piv[2][0] * new0 - piv[2][1] * new1
    left3 = line[3] - piv[3][0] * new0 - piv[3][1] * new1
    new2 = (rest[1][1] * left2 - rest[0][1] * left3) * inverse_rest
    new3 = (rest[0][0] * left3 - rest[1][0] * left2) * inverse_rest
    new0 = new0 - cross[0][0] * new2 - cross[1][0] * new3
    new1 = new1 - cross[0][1] * new2 - cross[1][1] * new3
    work = work - (cols[0] * new0 + cols[1] * new1) - (cols[2] * new2 + cols[3] * new3)
    for n, new in enumerate((new0, new1, new2, new3)):
        work = jnp.where(rows == step + n, new, work)
    return work


def final_kernel(
    mine_ref, other_ref, sol_ref, res_ref, dir_ref, image_ref, new_sol_ref, new_res_ref, new_dir_ref, gram
):
    rhs = 32
    half = mine_ref.shape[0]
    core = lax.axis_index("side")
    gram[pl.ds(pl.multiple_of(core * half, half), half), :] = mine_ref[...]
    gram[pl.ds(pl.multiple_of((1 - core) * half, half), half), :] = other_ref[...]
    total = gram[...]
    curv = total[:, 0:32]
    cross = total[:, 32:64]
    gram_image = total[:, 64:96]
    old_norm = total[:, 96:128]
    curv = 0.5 * (curv + curv.T)
    first = jnp.concatenate([curv, old_norm, cross, gram_image], axis=1)
    second = jnp.concatenate([old_norm, cross.T, jnp.zeros((rhs, 64), F32)], axis=1)
    for step in range(0, rhs, 4):
        first = eliminate(first, step)
        second = eliminate(second, step)
    alpha = first[:, 32:64]
    row = lax.broadcasted_iota(jnp.int32, (rhs, rhs), 0)
    col = lax.broadcasted_iota(jnp.int32, (rhs, rhs), 1)
    eye = (row == col).astype(F32)
    beta = eye - first[:, 64:96] + dot_f32(first[:, 96:128] - second[:, 32:64], alpha, ((1,), (0,)))
    direction = dir_ref[...]
    new_sol_ref[...] = sol_ref[...] + dot_f32(alpha, direction, ((0,), (0,)))
    new_res = res_ref[...] - dot_f32(alpha, image_ref[...], ((0,), (0,)))
    new_res_ref[...] = new_res
    new_dir_ref[...] = new_res + dot_f32(beta, direction, ((0,), (0,)))


def call(kernel, outs, ins, name, megabytes, scratch=(), space=pltpu.VMEM):
    return pl.pallas_call(
        kernel,
        out_shape=tuple(jax.ShapeDtypeStruct(*out) for out in outs),
        in_specs=[pl.BlockSpec(memory_space=space)] * len(ins),
        out_specs=(pl.BlockSpec(memory_space=pltpu.VMEM),) * len(outs),
        scratch_shapes=scratch,
        compiler_params=pltpu.CompilerParams(vmem_limit_bytes=megabytes << 20),
        name=name,
    )(*ins)


def per_device(chips, points, noise_var, district, solution, residual, direction):
    rhs, count = direction.shape
    whole_count = count * chips * 2
    group = ("row", "pair")
    swap = [(0, 1), (1, 0)]
    wide = ((rhs, count), F32)
    half = ((rhs // 2, LANES), F32)
    side = pltpu.VMEM((count, 40), BF16)
    gram = pltpu.VMEM((rhs, LANES), F32)
    fetched = (points, district.reshape(1, count), noise_var.reshape(1, count), direction)
    block, own = call(
        pack_kernel,
        (((ROWS, LANES), BF16), ((8, count), F32)),
        fetched,
        "pack", 4,
        [pltpu.VMEM(arg.shape, arg.dtype) for arg in fetched] + [pltpu.SemaphoreType.DMA((len(fetched),))],
        pltpu.HBM,
    )
    near = lax.all_to_all(jnp.broadcast_to(block[None], (chips, ROWS, LANES)), group, 0, 0)
    far = lax.ppermute(near, "side", swap)
    product, sums, norm = call(
        first_kernel,
        (wide, ((rhs + 8, count), F32), ((rhs, rhs), F32)),
        (own, direction, residual, near),
        "near_half", 24, [side],
    )
    image, keep, send = call(
        functools.partial(second_kernel, whole_count),
        (wide, half, half),
        (own, direction, residual, norm, product, sums, far),
        "far_half", 24, [side, gram],
    )
    chip_half = keep + lax.ppermute(send, "side", swap)
    halves = lax.all_to_all(jnp.broadcast_to(chip_half[None], (chips, *half[0])), group, 0, 0)
    mine = jnp.sum(halves, axis=0)
    other = lax.ppermute(mine, "side", swap)
    return call(
        final_kernel,
        (wide,) * 3,
        (mine, other, solution, residual, direction, image),
        "final", 8, [gram],
    )


def solution(mesh):
    rows, cols = mesh.shape["row"], mesh.shape["col"]
    paired = Mesh(mesh.devices.reshape(rows, cols // 2, 2), ("row", "pair", "side"))
    samples = ("row", "pair", "side")
    wide, flat = P(None, samples), P(samples)
    return jax.shard_map(
        functools.partial(per_device, rows * cols // 2),
        mesh=paired,
        in_specs=(wide, flat, flat, wide, wide, wide),
        out_specs=(wide, wide, wide),
        check_vma=False,
    )
```

time: 45.7 us -> 42.4 us (0.928)
  Pallas kernels: 9.84 us -> 7.26 us
  blocking collectives: 32.5 us -> 30 us
  waiting for transfers between devices: 0.85 us -> 1.99 us
  local copies, waits for them, and re-layouts: 0.8 us -> 1.51 us
    pallas_call x4, Pallas kernels: 9.84 us -> 7.26 us  [call(): pl.pallas_call(kernel, out_shape=tuple((jax.ShapeDtypeStruct(*out) for ou...]
    all_to_all x1, blocking collectives: 13.6 us -> 11.2 us  [per_device(): lax.all_to_all(jnp.broadcast_to(chip_half[None], (chips, *half[0])), grou...]
    unnamed x8 -> x14, local copies, waits for them, and re-layouts: 0.02 us -> 1.46 us
    ppermute x1 -> x2, waiting for transfers between devices: 0.84 us -> 1.99 us  [the longest x1 1.16 us: per_device(): other = lax.ppermute(mine, 'side', swap)]
    broadcast_in_dim x1, local copies, waits for them, and re-layouts: 0.76 us -> 0.04 us  [per_device(): jnp.broadcast_to(block[None], (chips, ROWS, LANES))]
  transfers between devices with their start and end apart: 2 -> 3, of which waited for: 1 -> 2; matrix products, arithmetic and copies ran while one was open for 0% -> 0% of each run, Pallas kernels for 5% -> 4%
where the time goes in v3:
time: 42.4 us; the launch traced here: 42.1 us
  blocking collectives  30 us (71%)
  Pallas kernels  7.26 us (17%)
  waiting for transfers between devices  1.99 us (5%)
  local copies, waits for them, and re-layouts  1.51 us (4%)
  between operations  0.71 us (2%)
  starting transfers between devices  0.6 us (1%)
    all_to_all x1, blocking collectives, per_device(): lax.all_to_all(jnp.broadcast_to(block[None], (chips, ROWS, LANES)), group...  18.8 us
    all_to_all x1, blocking collectives, per_device(): lax.all_to_all(jnp.broadcast_to(chip_half[None], (chips, *half[0])), grou...  11.2 us
    pallas_call x4, Pallas kernels, call(): pl.pallas_call(kernel, out_shape=tuple((jax.ShapeDtypeStruct(*out) for ou...  7.26 us
    unnamed x14, local copies, waits for them, and re-layouts  1.46 us
    ppermute x1, waiting for transfers between devices, per_device(): other = lax.ppermute(mine, 'side', swap)  1.16 us
  transfers between devices with their start and end apart: 3, of which 2 were waited for; matrix products, arithmetic and copies ran while one was open for 0% of the time, Pallas kernels for 4%

profile of v3, /device:TPU:0, one launch (start us, length us, event | category | flops | bytes accessed | tf_op | source)
XLA Modules:
  0.0 42.1 jit_solution(16174551046765195443)
XLA Ops:
  0.6 0.0 copy-start.5
  0.6 0.0 copy-start.6
  0.7 0.0 copy-start.4
  0.7 0.7 %copy-done.5 = s32[256]{0:T(256)S(1)} copy-done((s32[256]{0:T(256)S(1)}, s32[256]{0:T(256)}, u32[]{:S(2)}) %copy-start.5) | copy-done | bytes 1048
  1.3 0.0 copy-done.6
  1.3 0.0 copy-done.4
  1.3 0.0 copy-start
  1.3 0.8 %copy-done = f32[32,256]{1,0:T(8,128)S(1)} copy-done((f32[32,256]{1,0:T(8,128)S(1)}, f32[32,256]{1,0:T(8,128)}, u32[]{:S(2)}) %copy-start) | copy-done | bytes 32792
  2.1 0.5 %pack.1 = (bf16[72,128]{1,0:T(8,128)(2,1)S(1)}, f32[8,256]{1,0:T(8,128)S(1)}) custom-call(bf16[2,256]{1,0:T(2,128)(2,1)S(1)} %copy-done.4, s32[1,256]{1,0:T(1,128)S(1)} %bitcast.2, f32[1,256]{1,0:T(1,128)S(1)} %bitcast.3, f32[32,256]{1,0:T(8,128)S(1)} %copy-done), custom_call_target="tpu_custom_call" | custom-call | tf_op jit(solution)/shard_map/pack/pallas_call | solution.py:241
  2.6 0.0 copy-start.1
  2.6 0.0 copy-start.2
  2.7 18.8 %all_to_all.10.all_ref = bf16[16,72,128]{2,1,0:T(8,128)(2,1)S(1)} all-to-all(bf16[16,72,128]{2,1,0:T(8,128)(2,1)S(1)} %broadcast_in_dim.4), channel_id=1, replica_groups=mesh['row'=4,'pair'=4,'side'=2] {'row','pair'}, dimensions={0} | all-to-all | bytes 589824 | tf_op jit(solution)/shard_map/all_to_all | solution.py:270
  21.5 0.0 collective-permute-start
  21.5 0.0 copy-done.1
  21.5 0.0 copy-done.2
  21.5 1.8 %near_half.1 = (f32[32,256]{1,0:T(8,128)S(1)}, f32[40,256]{1,0:T(8,128)S(1)}, f32[32,32]{1,0:T(8,128)S(1)}) custom-call(f32[8,256]{1,0:T(8,128)S(1)} %get-tuple-element.11.own_ref, f32[32,256]{1,0:T(8,128)S(1)} %copy-done.1, f32[32,256]{1,0:T(8,128)S(1)} %copy-done.2, bf16[16,72,128]{2,1,0:T(8,128)(2,1)S(1)} %all_to_all.10.all_ref), custom_call_target="tpu_custom_call" | custom-call | tf_op jit(solution)/shard_map/near_half/pallas_call | solution.py:241
  23.3 0.0 collective-permute-done.all_ref
  23.3 2.5 %far_half.1 = (f32[32,256]{1,0:T(8,128)S(1)}, f32[16,128]{1,0:T(8,128)S(1)}, f32[16,128]{1,0:T(8,128)S(1)}) custom-call(f32[8,256]{1,0:T(8,128)S(1)} %get-tuple-element.11.own_ref, f32[32,256]{1,0:T(8,128)S(1)} %copy-done.1, f32[32,256]{1,0:T(8,128)S(1)} %copy-done.2, f32[32,32]{1,0:T(8,128)S(1)} %get-tuple-element.13.norm_ref, ...), custom_call_target="tpu_custom_call" | custom-call | tf_op jit(solution)/shard_map/far_half/pallas_call | solution.py:241
  25.8 0.5 %collective-permute-start.1 = (f32[16,128]{1,0:T(8,128)S(1)}, f32[16,128]{1,0:T(8,128)S(1)}, u32[]{:S(2)}, u32[]{:S(2)}) collective-permute-start(f32[16,128]{1,0:T(8,128)S(1)} %get-tuple-element.17), channel_id=1, source_target_pairs={{0,1},{1,0},{2,3},{3,2},{4,5},{5,4},{6,7},{7,6},{8,9},{9,8},{10,11... | collective-permute-start | bytes 24584 | tf_op jit(solution)/shard_map/ppermute | solution.py:284
  26.3 0.8 %collective-permute-done.1 = f32[16,128]{1,0:T(8,128)S(1)} collective-permute-done((f32[16,128]{1,0:T(8,128)S(1)}, f32[16,128]{1,0:T(8,128)S(1)}, u32[]{:S(2)}, u32[]{:S(2)}) %collective-permute-start.1) | collective-permute-done | bytes 8224 | tf_op jit(solution)/shard_map/ppermute | solution.py:284
  27.2 11.2 %all_to_all.11 = f32[16,16,128]{2,1,0:T(8,128)S(1)} all-to-all(f32[16,16,128]{2,1,0:T(8,128)S(1)} %broadcast_in_dim.5), channel_id=1, replica_groups=mesh['row'=4,'pair'=4,'side'=2] {'row','pair'}, dimensions={0} | all-to-all | bytes 262144 | tf_op jit(solution)/shard_map/all_to_all | solution.py:285
  38.4 0.0 copy-start.3
  38.4 0.1 collective-permute-start.2
  38.5 1.2 %collective-permute-done.2.other_ref = f32[16,128]{1,0:T(8,128)S(1)} collective-permute-done((f32[16,128]{1,0:T(8,128)S(1)}, f32[16,128]{1,0:T(8,128)S(1)}, u32[]{:S(2)}, u32[]{:S(2)}) %collective-permute-start.2) | collective-permute-done | bytes 8224 | tf_op jit(solution)/shard_map/ppermute | solution.py:287
  39.6 0.0 copy-done.3
  39.6 2.4 %final.1 = (f32[32,256]{1,0:T(8,128)}, f32[32,256]{1,0:T(8,128)}, f32[32,256]{1,0:T(8,128)}) custom-call(f32[16,128]{1,0:T(8,128)S(1)} %reduce_sum.9.mine_ref, f32[16,128]{1,0:T(8,128)S(1)} %collective-permute-done.2.other_ref, f32[32,256]{1,0:T(8,128)S(1)} %copy-done.3, f32[32,256]{1,0:T(8,128)S(1)} %copy-done.2, f32[32,256]{1,0:T(8,128)S(1)} %copy-done.1, ...), custom_call_target="tpu_custom_call" | custom-call | tf_op jit(solution)/shard_map/final/pallas_call | solution.py:241
  (4 shorter events, 0.1 us)
Async XLA Ops:
  0.6 0.7 %copy-start.5 = (s32[256]{0:T(256)S(1)}, s32[256]{0:T(256)}, u32[]{:S(2)}) copy-start(s32[256]{0:T(256)} %param.8) | copy-start | bytes 3076
  0.6 0.7 %copy-start.6 = (f32[256]{0:T(256)S(1)}, f32[256]{0:T(256)}, u32[]{:S(2)}) copy-start(f32[256]{0:T(256)} %param.7) | copy-start | bytes 3076
  0.7 0.7 %copy-start.4 = (bf16[2,256]{1,0:T(2,128)(2,1)S(1)}, bf16[2,256]{1,0:T(2,128)(2,1)}, u32[]{:S(2)}) copy-start(bf16[2,256]{1,0:T(2,128)(2,1)} %points_hbm.1) | copy-start | bytes 3076
  1.3 0.8 %copy-start = (f32[32,256]{1,0:T(8,128)S(1)}, f32[32,256]{1,0:T(8,128)}, u32[]{:S(2)}) copy-start(f32[32,256]{1,0:T(8,128)} %dir_ref.5) | copy-start | bytes 98308
  2.6 18.8 %copy-start.1 = (f32[32,256]{1,0:T(8,128)S(1)}, f32[32,256]{1,0:T(8,128)}, u32[]{:S(2)}) copy-start(f32[32,256]{1,0:T(8,128)} %dir_ref.5) | copy-start | bytes 98308
  2.6 18.8 %copy-start.2 = (f32[32,256]{1,0:T(8,128)S(1)}, f32[32,256]{1,0:T(8,128)}, u32[]{:S(2)}) copy-start(f32[32,256]{1,0:T(8,128)} %res_ref.5) | copy-start | bytes 98308
  21.5 1.8 %collective-permute-start = (bf16[16,72,128]{2,1,0:T(8,128)(2,1)S(1)}, bf16[16,72,128]{2,1,0:T(8,128)(2,1)S(1)}, u32[]{:S(2)}, u32[]{:S(2)}) collective-permute-start(bf16[16,72,128]{2,1,0:T(8,128)(2,1)S(1)} %all_to_all.10.all_ref), channel_id=1, source_target_pairs={{0,1},{1,0},{2,3},{3,2},{4,5},{5,4},{6,7},{7,6},{8,9},{9,8},{10,11... | collective-permute-start | bytes 884744 | tf_op jit(solution)/shard_map/ppermute | solution.py:271
  25.8 1.4 %collective-permute-start.1 = (f32[16,128]{1,0:T(8,128)S(1)}, f32[16,128]{1,0:T(8,128)S(1)}, u32[]{:S(2)}, u32[]{:S(2)}) collective-permute-start(f32[16,128]{1,0:T(8,128)S(1)} %get-tuple-element.17), channel_id=1, source_target_pairs={{0,1},{1,0},{2,3},{3,2},{4,5},{5,4},{6,7},{7,6},{8,9},{9,8},{10,11... | collective-permute-start | bytes 24584 | tf_op jit(solution)/shard_map/ppermute | solution.py:284
  38.4 1.3 %copy-start.3 = (f32[32,256]{1,0:T(8,128)S(1)}, f32[32,256]{1,0:T(8,128)}, u32[]{:S(2)}) copy-start(f32[32,256]{1,0:T(8,128)} %sol_ref.1) | copy-start | bytes 98308
  38.4 1.2 %collective-permute-start.2 = (f32[16,128]{1,0:T(8,128)S(1)}, f32[16,128]{1,0:T(8,128)S(1)}, u32[]{:S(2)}, u32[]{:S(2)}) collective-permute-start(f32[16,128]{1,0:T(8,128)S(1)} %reduce_sum.9.mine_ref), channel_id=1, source_target_pairs={{0,1},{1,0},{2,3},{3,2},{4,5},{5,4},{6,7},{7,6},{8,9},{9,8},{10,11... | collective-permute-start | bytes 24584 | tf_op jit(solution)/shard_map/ppermute | solution.py:287

commit v4 on v3

--- a/solution.py
+++ b/solution.py
@@ -55,28 +55,23 @@
     own_ref[...] = jnp.concatenate(
         [pts, dist.astype(F32), noise_ref[...], jnp.zeros((4, count), F32)], axis=0
     )
-    stacked = stack_pieces(dir_ref[...])
-    high = stacked[0:rhs]
+    high, mid, low = three_pieces(dir_ref[...])
     first = dist[:, 0:1]
     last = dist[:, count - 1 : count]
     row = lax.broadcasted_iota(jnp.int32, (8, count), 0)
     picked = jnp.where(row == 0, first, last)
     wanted = (row == 0) | ((row == 1) & (first != last))
     mask = (wanted & (dist == picked)).astype(F32).astype(BF16)
-    edge = dot_bf16(mask, stacked, ((1,), (1,)))
-    total = edge + pltpu.roll(edge, LANES - rhs, 1) + pltpu.roll(edge, LANES - 2 * rhs, 1)
+    ones = jnp.ones((LANES - 3 * rhs, count), BF16)
+    edge = dot_bf16(mask, jnp.concatenate([high, high, high, ones], axis=0), ((1,), (1,)))
+    edge = edge + dot_bf16(mask, jnp.concatenate([mid, mid, mid, 0 * ones], axis=0), ((1,), (1,)))
+    edge = edge + dot_bf16(mask, jnp.concatenate([low, low, low, 0 * ones], axis=0), ((1,), (1,)))
+    e_high, e_mid, e_low = (piece.astype(F32) for piece in three_pieces(edge))
     lane = lax.broadcasted_iota(jnp.int32, (8, LANES), 1)
-    total = jnp.where(lane < rhs, total, 0.0)
-    e_high, e_mid, e_low = three_pieces(total)
     row8 = lax.broadcasted_iota(jnp.int32, (8, LANES), 0)
     label = jnp.where(row8 == 0, first, last).astype(F32)
-    extras = (
-        e_high.astype(F32)
-        + pltpu.roll(e_mid.astype(F32), rhs, 1)
-        + pltpu.roll(e_low.astype(F32), 2 * rhs, 1)
-    )
-    extras = jnp.where(lane == 3 * rhs, label, extras)
-    extras = jnp.where(lane == 3 * rhs + 1, edge, extras)
+    extras = jnp.where(lane < rhs, e_high, jnp.where(lane < 2 * rhs, e_mid, e_low))
+    extras = jnp.where(lane == 3 * rhs, label, jnp.where(lane > 3 * rhs, edge, extras))
     tail = jnp.concatenate(
         [pts[:, 0:LANES], pts[:, LANES:], extras[0:2, :], jnp.zeros((2, LANES), F32)], axis=0
     )
@@ -111,8 +106,6 @@
     blocks = all_ref.shape[0]
     count = own_ref.shape[1]
     rhs = 32
-    own = own_ref[...]
-    side[...] = own_side(own).T.astype(BF16)
     to_two = -math.log2(math.e)
 
     def one_block(index, acc):
@@ -140,15 +133,16 @@
     place = lax.broadcasted_iota(jnp.int32, (blocks * 8, count), 0)
     kind = place % 8
     good = ((kind == 4) | (kind == 5)) & (place // 8 != skip)
-    match = good & (edges[:, 3 * rhs : 3 * rhs + 1] == own[2:3, :])
+    match = good & (edges[:, 3 * rhs : 3 * rhs + 1] == own_ref[2:3, :])
     sums = dot_bf16(edges.astype(BF16), match.astype(F32).astype(BF16), ((0,), (0,)))
     extra = sums[0:rhs] + sums[rhs : 2 * rhs] + sums[2 * rhs : 3 * rhs]
     return product, extra, sums[3 * rhs + 1 : 3 * rhs + 2]
 
 
-def first_kernel(own_ref, dir_ref, res_ref, all_ref, product_ref, sums_ref, norm_ref, side):
+def first_kernel(own_ref, dir_ref, res_ref, all_ref, product_ref, sums_ref, norm_ref, side_ref):
     rhs, count = dir_ref.shape
-    product, extra, number = half_product(lax.axis_index(("row", "pair")), own_ref, all_ref, side)
+    side_ref[...] = own_side(own_ref[...]).T.astype(BF16)
+    product, extra, number = half_product(lax.axis_index(("row", "pair")), own_ref, all_ref, side_ref)
     product_ref[...] = product
     labels = lax.broadcasted_iota(jnp.int32, (64, count), 0).astype(F32)
     onehot = (labels == own_ref[2:3, :]).astype(F32).astype(BF16)
@@ -156,14 +150,16 @@
     sums = dot_bf16(stack_pieces(dir_ref[...]), same, ((1,), (0,)))
     sums_ref[0:rhs, :] = sums[0:rhs] + sums[rhs : 2 * rhs] + sums[2 * rhs : 3 * rhs] + extra
     sums_ref[rhs:, :] = sums[3 * rhs : 3 * rhs + 8] + number
-    norm_ref[...] = dot_f32(res_ref[...], res_ref[...], ((1,), (1,)))
+    residual = res_ref[...]
+    norm_ref[...] = jnp.zeros_like(norm_ref)
+    norm_ref[:, 32:64] = dot_f32(residual, residual, ((1,), (1,)))
 
 
 def second_kernel(
-    whole_count, own_ref, dir_ref, res_ref, norm_ref, product_ref, sums_ref, all_ref,
-    image_ref, keep_ref, send_ref, side, gram,
+    whole_count, own_ref, dir_ref, res_ref, norm_ref, product_ref, sums_ref, side_ref, all_ref,
+    image_ref, keep_ref, send_ref,
 ):
-    product, extra, number = half_product(-1, own_ref, all_ref, side)
+    product, extra, number = half_product(-1, own_ref, all_ref, side_ref)
     product = product + product_ref[...]
     size = sums_ref[32:33, :] + number
     district_part = (sums_ref[0:32, :] + extra) / jnp.sqrt(size)
@@ -171,13 +167,15 @@
     kernel_scale = 1.0 / (corr_range * math.sqrt(whole_count))
     image = own_ref[3:4, :] * direction + product * kernel_scale + district_gain * district_part
     image_ref[...] = image
-    right = jnp.concatenate([direction, res_ref[...], image], axis=0)
-    gram[:, 0:96] = dot_f32(image, right, ((1,), (1,)))
-    gram[:, 96:128] = norm_ref[...]
+    part = 0.5 * direction
+    none = jnp.zeros_like(part)
+    gram = dot_f32(image, jnp.concatenate([part, none, res_ref[...], image], axis=0), ((1,), (1,)))
+    gram = gram + dot_f32(part, jnp.concatenate([image, none, none, none], axis=0), ((1,), (1,)))
+    gram = gram + norm_ref[...]
     half = keep_ref.shape[0]
-    core = lax.axis_index("side")
-    keep_ref[...] = gram[pl.ds(pl.multiple_of(core * half, half), half), :]
-    send_ref[...] = gram[pl.ds(pl.multiple_of((1 - core) * half, half), half), :]
+    even = lax.axis_index("side") == 0
+    keep_ref[...] = jnp.where(even, gram[:half], gram[half:])
+    send_ref[...] = jnp.where(even, gram[half:], gram[:half])
 
 
 def eliminate(work, step):
@@ -206,22 +204,12 @@
     return work
 
 
-def final_kernel(
-    mine_ref, other_ref, sol_ref, res_ref, dir_ref, image_ref, new_sol_ref, new_res_ref, new_dir_ref, gram
-):
-    rhs = 32
-    half = mine_ref.shape[0]
-    core = lax.axis_index("side")
-    gram[pl.ds(pl.multiple_of(core * half, half), half), :] = mine_ref[...]
-    gram[pl.ds(pl.multiple_of((1 - core) * half, half), half), :] = other_ref[...]
-    total = gram[...]
-    curv = total[:, 0:32]
-    cross = total[:, 32:64]
-    gram_image = total[:, 64:96]
-    old_norm = total[:, 96:128]
-    curv = 0.5 * (curv + curv.T)
-    first = jnp.concatenate([curv, old_norm, cross, gram_image], axis=1)
-    second = jnp.concatenate([old_norm, cross.T, jnp.zeros((rhs, 64), F32)], axis=1)
+def final_kernel(mine_ref, other_ref, sol_ref, res_ref, dir_ref, image_ref, new_sol_ref, new_res_ref, new_dir_ref):
+    rhs = sol_ref.shape[0]
+    mine, other = mine_ref[...], other_ref[...]
+    even = lax.axis_index("side") == 0
+    first = jnp.concatenate([jnp.where(even, mine, other), jnp.where(even, other, mine)], axis=0)
+    second = jnp.concatenate([first[:, 32:64], first[:, 64:96].T, jnp.zeros((rhs, 64), F32)], axis=1)
     for step in range(0, rhs, 4):
         first = eliminate(first, step)
         second = eliminate(second, step)
@@ -256,9 +244,8 @@
     swap = [(0, 1), (1, 0)]
     wide = ((rhs, count), F32)
     half = ((rhs // 2, LANES), F32)
-    side = pltpu.VMEM((count, 40), BF16)
-    gram = pltpu.VMEM((rhs, LANES), F32)
     fetched = (points, district.reshape(1, count), noise_var.reshape(1, count), direction)
+    fetched = tuple(pltpu.with_memory_space_constraint(arg, pltpu.HBM) for arg in fetched)
     block, own = call(
         pack_kernel,
         (((ROWS, LANES), BF16), ((8, count), F32)),
@@ -269,17 +256,17 @@
     )
     near = lax.all_to_all(jnp.broadcast_to(block[None], (chips, ROWS, LANES)), group, 0, 0)
     far = lax.ppermute(near, "side", swap)
-    product, sums, norm = call(
+    product, sums, norm, side = call(
         first_kernel,
-        (wide, ((rhs + 8, count), F32), ((rhs, rhs), F32)),
+        (wide, ((rhs + 8, count), F32), ((rhs, LANES), F32), ((count, 40), BF16)),
         (own, direction, residual, near),
-        "near_half", 24, [side],
+        "near_half", 24,
     )
     image, keep, send = call(
         functools.partial(second_kernel, whole_count),
         (wide, half, half),
-        (own, direction, residual, norm, product, sums, far),
-        "far_half", 24, [side, gram],
+        (own, direction, residual, norm, product, sums, side, far),
+        "far_half", 24,
     )
     chip_half = keep + lax.ppermute(send, "side", swap)
     halves = lax.all_to_all(jnp.broadcast_to(chip_half[None], (chips, *half[0])), group, 0, 0)
@@ -289,7 +276,7 @@
         final_kernel,
         (wide,) * 3,
         (mine, other, solution, residual, direction, image),
-        "final", 8, [gram],
+        "final", 8,
     )
 
 

time: 42.4 us -> 40.9 us (0.965)
  local copies, waits for them, and re-layouts: 1.51 us -> 0.07 us
    unnamed x14 -> x6, local copies, waits for them, and re-layouts: 1.46 us -> 0.02 us
  transfers between devices with their start and end apart: 3 -> 3, of which waited for: 2 -> 2; matrix products, arithmetic and copies ran while one was open for 0% -> 0% of each run, Pallas kernels for 4% -> 5%
where the time goes in v4:
time: 40.9 us; the launch traced here: 40.6 us
  blocking collectives  30 us (73%)
  Pallas kernels  7.25 us (18%)
  waiting for transfers between devices  1.99 us (5%)
  between operations  0.68 us (2%)
  starting transfers between devices  0.63 us (2%)
    all_to_all x1, blocking collectives, per_device(): lax.all_to_all(jnp.broadcast_to(block[None], (chips, ROWS, LANES)), group...  18.8 us
    all_to_all x1, blocking collectives, per_device(): lax.all_to_all(jnp.broadcast_to(chip_half[None], (chips, *half[0])), grou...  11.2 us
    pallas_call x4, Pallas kernels, call(): pl.pallas_call(kernel, out_shape=tuple((jax.ShapeDtypeStruct(*out) for ou...  7.25 us
    ppermute x1, waiting for transfers between devices, per_device(): other = lax.ppermute(mine, 'side', swap)  1.16 us
    ppermute x1, waiting for transfers between devices, per_device(): chip_half = keep + lax.ppermute(send, 'side', swap)  0.83 us
  transfers between devices with their start and end apart: 3, of which 2 were waited for; matrix products, arithmetic and copies ran while one was open for 0% of the time, Pallas kernels for 5%

profile of v4, /device:TPU:0, one launch (start us, length us, event | category | flops | bytes accessed | tf_op | source)
XLA Modules:
  0.0 40.6 jit_solution(14428705643101029838)
XLA Ops:
  0.6 1.1 %pack.1 = (bf16[72,128]{1,0:T(8,128)(2,1)S(1)}, f32[8,256]{1,0:T(8,128)S(1)}) custom-call(bf16[2,256]{1,0:T(2,128)(2,1)} %points_hbm.1, s32[1,256]{1,0:T(1,128)} %bitcast.2, f32[1,256]{1,0:T(1,128)} %bitcast.3, f32[32,256]{1,0:T(8,128)} %dir_ref.5), custom_call_target="tpu_custom_call" | custom-call | tf_op jit(solution)/shard_map/pack/pallas_call | solution.py:229
  1.8 0.0 copy-start
  1.8 0.0 copy-start.1
  1.8 18.8 %all_to_all.10.all_ref = bf16[16,72,128]{2,1,0:T(8,128)(2,1)S(1)} all-to-all(bf16[16,72,128]{2,1,0:T(8,128)(2,1)S(1)} %broadcast_in_dim.4), channel_id=1, replica_groups=mesh['row'=4,'pair'=4,'side'=2] {'row','pair'}, dimensions={0} | all-to-all | bytes 589824 | tf_op jit(solution)/shard_map/all_to_all | solution.py:257
  20.6 0.0 collective-permute-start
  20.6 0.0 copy-done
  20.6 0.0 copy-done.1
  20.7 1.9 %near_half.1 = (f32[32,256]{1,0:T(8,128)S(1)}, f32[40,256]{1,0:T(8,128)S(1)}, f32[32,128]{1,0:T(8,128)S(1)}, bf16[256,40]{1,0:T(8,128)(2,1)S(1)}) custom-call(f32[8,256]{1,0:T(8,128)S(1)} %get-tuple-element.12.own_ref, f32[32,256]{1,0:T(8,128)S(1)} %copy-done, f32[32,256]{1,0:T(8,128)S(1)} %copy-done.1, bf16[16,72,128]{2,1,0:T(8,128)(2,1)S(1)} %all_to_all.10.all_ref), custom_call_target="tpu_custom_call" | custom-call | tf_op jit(solution)/shard_map/near_half/pallas_call | solution.py:229
  22.5 0.0 collective-permute-done.all_ref
  22.5 1.8 %far_half.1 = (f32[32,256]{1,0:T(8,128)S(1)}, f32[16,128]{1,0:T(8,128)S(1)}, f32[16,128]{1,0:T(8,128)S(1)}) custom-call(f32[8,256]{1,0:T(8,128)S(1)} %get-tuple-element.12.own_ref, f32[32,256]{1,0:T(8,128)S(1)} %copy-done, f32[32,256]{1,0:T(8,128)S(1)} %copy-done.1, f32[32,128]{1,0:T(8,128)S(1)} %get-tuple-element.14.norm_ref, ...), custom_call_target="tpu_custom_call" | custom-call | tf_op jit(solution)/shard_map/far_half/pallas_call | solution.py:229
  24.4 0.6 %collective-permute-start.1 = (f32[16,128]{1,0:T(8,128)S(1)}, f32[16,128]{1,0:T(8,128)S(1)}, u32[]{:S(2)}, u32[]{:S(2)}) collective-permute-start(f32[16,128]{1,0:T(8,128)S(1)} %get-tuple-element.19), channel_id=1, source_target_pairs={{0,1},{1,0},{2,3},{3,2},{4,5},{5,4},{6,7},{7,6},{8,9},{9,8},{10,11... | collective-permute-start | bytes 24584 | tf_op jit(solution)/shard_map/ppermute | solution.py:271
  24.9 0.8 %collective-permute-done.1 = f32[16,128]{1,0:T(8,128)S(1)} collective-permute-done((f32[16,128]{1,0:T(8,128)S(1)}, f32[16,128]{1,0:T(8,128)S(1)}, u32[]{:S(2)}, u32[]{:S(2)}) %collective-permute-start.1) | collective-permute-done | bytes 8224 | tf_op jit(solution)/shard_map/ppermute | solution.py:271
  25.8 11.2 %all_to_all.11 = f32[16,16,128]{2,1,0:T(8,128)S(1)} all-to-all(f32[16,16,128]{2,1,0:T(8,128)S(1)} %broadcast_in_dim.5), channel_id=1, replica_groups=mesh['row'=4,'pair'=4,'side'=2] {'row','pair'}, dimensions={0} | all-to-all | bytes 262144 | tf_op jit(solution)/shard_map/all_to_all | solution.py:272
  36.9 0.0 copy-start.2
  37.0 0.1 collective-permute-start.2
  37.0 1.2 %collective-permute-done.2.other_ref = f32[16,128]{1,0:T(8,128)S(1)} collective-permute-done((f32[16,128]{1,0:T(8,128)S(1)}, f32[16,128]{1,0:T(8,128)S(1)}, u32[]{:S(2)}, u32[]{:S(2)}) %collective-permute-start.2) | collective-permute-done | bytes 8224 | tf_op jit(solution)/shard_map/ppermute | solution.py:274
  38.2 0.0 copy-done.2
  38.2 2.4 %final.1 = (f32[32,256]{1,0:T(8,128)}, f32[32,256]{1,0:T(8,128)}, f32[32,256]{1,0:T(8,128)}) custom-call(f32[16,128]{1,0:T(8,128)S(1)} %reduce_sum.9.mine_ref, f32[16,128]{1,0:T(8,128)S(1)} %collective-permute-done.2.other_ref, f32[32,256]{1,0:T(8,128)S(1)} %copy-done.2, f32[32,256]{1,0:T(8,128)S(1)} %copy-done.1, f32[32,256]{1,0:T(8,128)S(1)} %copy-done, ...), custom_call_target="tpu_custom_call" | custom-call | tf_op jit(solution)/shard_map/final/pallas_call | solution.py:229
  (4 shorter events, 0.1 us)
Async XLA Ops:
  1.8 18.8 %copy-start = (f32[32,256]{1,0:T(8,128)S(1)}, f32[32,256]{1,0:T(8,128)}, u32[]{:S(2)}) copy-start(f32[32,256]{1,0:T(8,128)} %dir_ref.5) | copy-start | bytes 98308
  1.8 18.8 %copy-start.1 = (f32[32,256]{1,0:T(8,128)S(1)}, f32[32,256]{1,0:T(8,128)}, u32[]{:S(2)}) copy-start(f32[32,256]{1,0:T(8,128)} %res_ref.5) | copy-start | bytes 98308
  20.6 1.9 %collective-permute-start = (bf16[16,72,128]{2,1,0:T(8,128)(2,1)S(1)}, bf16[16,72,128]{2,1,0:T(8,128)(2,1)S(1)}, u32[]{:S(2)}, u32[]{:S(2)}) collective-permute-start(bf16[16,72,128]{2,1,0:T(8,128)(2,1)S(1)} %all_to_all.10.all_ref), channel_id=1, source_target_pairs={{0,1},{1,0},{2,3},{3,2},{4,5},{5,4},{6,7},{7,6},{8,9},{9,8},{10,11... | collective-permute-start | bytes 884744 | tf_op jit(solution)/shard_map/ppermute | solution.py:258
  24.4 1.4 %collective-permute-start.1 = (f32[16,128]{1,0:T(8,128)S(1)}, f32[16,128]{1,0:T(8,128)S(1)}, u32[]{:S(2)}, u32[]{:S(2)}) collective-permute-start(f32[16,128]{1,0:T(8,128)S(1)} %get-tuple-element.19), channel_id=1, source_target_pairs={{0,1},{1,0},{2,3},{3,2},{4,5},{5,4},{6,7},{7,6},{8,9},{9,8},{10,11... | collective-permute-start | bytes 24584 | tf_op jit(solution)/shard_map/ppermute | solution.py:271
  36.9 1.3 %copy-start.2 = (f32[32,256]{1,0:T(8,128)S(1)}, f32[32,256]{1,0:T(8,128)}, u32[]{:S(2)}) copy-start(f32[32,256]{1,0:T(8,128)} %sol_ref.1) | copy-start | bytes 98308
  37.0 1.2 %collective-permute-start.2 = (f32[16,128]{1,0:T(8,128)S(1)}, f32[16,128]{1,0:T(8,128)S(1)}, u32[]{:S(2)}, u32[]{:S(2)}) collective-permute-start(f32[16,128]{1,0:T(8,128)S(1)} %reduce_sum.9.mine_ref), channel_id=1, source_target_pairs={{0,1},{1,0},{2,3},{3,2},{4,5},{5,4},{6,7},{7,6},{8,9},{9,8},{10,11... | collective-permute-start | bytes 24584 | tf_op jit(solution)/shard_map/ppermute | solution.py:274

commit v5 on v4

--- a/solution.py
+++ b/solution.py
@@ -157,7 +157,7 @@
 
 def second_kernel(
     whole_count, own_ref, dir_ref, res_ref, norm_ref, product_ref, sums_ref, side_ref, all_ref,
-    image_ref, keep_ref, send_ref,
+    image_ref, packed_ref,
 ):
     product, extra, number = half_product(-1, own_ref, all_ref, side_ref)
     product = product + product_ref[...]
@@ -172,10 +172,55 @@
     gram = dot_f32(image, jnp.concatenate([part, none, res_ref[...], image], axis=0), ((1,), (1,)))
     gram = gram + dot_f32(part, jnp.concatenate([image, none, none, none], axis=0), ((1,), (1,)))
     gram = gram + norm_ref[...]
-    half = keep_ref.shape[0]
-    even = lax.axis_index("side") == 0
-    keep_ref[...] = jnp.where(even, gram[:half], gram[half:])
-    send_ref[...] = jnp.where(even, gram[half:], gram[:half])
+    packed = pack_gram(gram)
+    for n in range(6):
+        packed_ref[n] = packed[n // 2][4 * (n % 2) : 4 * (n % 2) + 4, :]
+
+
+def lane_groups(height):
+    row = lax.broadcasted_iota(jnp.int32, (height, LANES), 0)
+    lane = lax.broadcasted_iota(jnp.int32, (height, LANES), 1)
+    return row, lane % 32, lane // 32
+
+
+def pack_gram(gram):
+    row, col, group = lane_groups(32)
+    below = (col <= row) & (group <= 1)
+    kept = jnp.where(below | (group == 2) | ((group == 3) & (col > row)), gram, 0.0)
+    diag = jnp.sum(jnp.where((group == 3) & (col == row), gram, 0.0), axis=0, keepdims=True)
+    diag = jnp.broadcast_to(diag, (8, LANES))
+    row8, col8, group8 = lane_groups(8)
+    packed = [jnp.zeros((8, LANES), F32)] * 3
+    for n in range(4):
+        rows = kept[8 * n : 8 * n + 8]
+        for source, target in ((0, 1), (1, 2), (2, 0), (3, 1)):
+            turn = (n - source) % 4 * 32
+            moved = pltpu.roll(rows, turn, 1) if turn else rows
+            packed[target] = packed[target] + jnp.where(group8 == n, moved, 0.0)
+    packed[2] = packed[2] + jnp.where((group8 == 0) & (row8 == 0) & (col8 > 0), pltpu.roll(diag, 32, 1), 0.0)
+    packed[2] = packed[2] + jnp.where((group8 == 0) & (row8 == 1) & (col8 == 2), pltpu.roll(diag, 34, 1), 0.0)
+    return packed
+
+
+def unpack_gram(packed):
+    _, _, group8 = lane_groups(8)
+    parts = []
+    for n in range(4):
+        rows = jnp.zeros((8, LANES), F32)
+        for source, target in ((0, 1), (1, 2), (2, 0), (3, 1)):
+            turn = (source - n) % 4 * 32
+            moved = pltpu.roll(packed[target], turn, 1) if turn else packed[target]
+            rows = jnp.where(group8 == source, moved, rows)
+        parts.append(rows)
+    flat = jnp.concatenate(parts, axis=0)
+    turned = flat.T
+    turned = jnp.concatenate([turned[0:32], turned[32:64], turned[64:96], turned[96:128]], axis=1)
+    row, col, group = lane_groups(32)
+    diag = jnp.where(col[0:1] == 0, pltpu.roll(flat[0:8], 62, 1)[1:2], pltpu.roll(flat[0:8], 64, 1)[0:1])
+    direct = (group == 2) | ((group <= 1) & (col <= row)) | ((group == 3) & (col > row))
+    first = jnp.where(direct, flat, jnp.where((group == 3) & (col == row), diag, turned))
+    second = pltpu.roll(jnp.where(group == 1, first, turned), 96, 1)
+    return first, second
 
 
 def eliminate(work, step):
@@ -206,10 +251,10 @@
 
 def final_kernel(mine_ref, other_ref, sol_ref, res_ref, dir_ref, image_ref, new_sol_ref, new_res_ref, new_dir_ref):
     rhs = sol_ref.shape[0]
-    mine, other = mine_ref[...], other_ref[...]
     even = lax.axis_index("side") == 0
-    first = jnp.concatenate([jnp.where(even, mine, other), jnp.where(even, other, mine)], axis=0)
-    second = jnp.concatenate([first[:, 32:64], first[:, 64:96].T, jnp.zeros((rhs, 64), F32)], axis=1)
+    quarters = [jnp.where(even, mine_ref[n], other_ref[n]) for n in range(3)]
+    quarters += [jnp.where(even, other_ref[n], mine_ref[n]) for n in range(3)]
+    first, second = unpack_gram([jnp.concatenate(quarters[2 * n : 2 * n + 2], axis=0) for n in range(3)])
     for step in range(0, rhs, 4):
         first = eliminate(first, step)
         second = eliminate(second, step)
@@ -243,7 +288,6 @@
     group = ("row", "pair")
     swap = [(0, 1), (1, 0)]
     wide = ((rhs, count), F32)
-    half = ((rhs // 2, LANES), F32)
     fetched = (points, district.reshape(1, count), noise_var.reshape(1, count), direction)
     fetched = tuple(pltpu.with_memory_space_constraint(arg, pltpu.HBM) for arg in fetched)
     block, own = call(
@@ -262,15 +306,14 @@
         (own, direction, residual, near),
         "near_half", 24,
     )
-    image, keep, send = call(
+    image, packed = call(
         functools.partial(second_kernel, whole_count),
-        (wide, half, half),
+        (wide, ((6, 4, LANES), F32)),
         (own, direction, residual, norm, product, sums, side, far),
         "far_half", 24,
     )
-    chip_half = keep + lax.ppermute(send, "side", swap)
-    halves = lax.all_to_all(jnp.broadcast_to(chip_half[None], (chips, *half[0])), group, 0, 0)
-    mine = jnp.sum(halves, axis=0)
+    copies = jnp.broadcast_to(packed.reshape(1, 2, 3, 4, LANES), (chips, 2, 3, 4, LANES)).reshape(-1, 3, 4, LANES)
+    mine = jnp.sum(lax.all_to_all(copies, group + ("side",), 0, 0, tiled=True), axis=0)
     other = lax.ppermute(mine, "side", swap)
     return call(
         final_kernel,

time: 40.9 us -> 40 us (0.978)
  waiting for transfers between devices: 1.99 us -> 0.83 us
    ppermute x1 -> x0, waiting for transfers between devices: 0.83 us -> none  [per_device(): chip_half = keep + lax.ppermute(send, 'side', swap)]
    ppermute x1, starting transfers between devices: 0.07 us -> 0.65 us  [per_device(): other = lax.ppermute(mine, 'side', swap)]
    ppermute x1 -> x0, starting transfers between devices: 0.55 us -> none  [per_device(): chip_half = keep + lax.ppermute(send, 'side', swap)]
  transfers between devices with their start and end apart: 3 -> 2, of which waited for: 2 -> 1; matrix products, arithmetic and copies ran while one was open for 0% -> 0% of each run, Pallas kernels for 5% -> 5%
where the time goes in v5:
time: 40 us; the launch traced here: 39.8 us
  blocking collectives  30 us (75%)
  Pallas kernels  7.43 us (19%)
  waiting for transfers between devices  0.83 us (2%)
  between operations  0.69 us (2%)
  starting transfers between devices  0.66 us (2%)
    all_to_all x1, blocking collectives, per_device(): lax.all_to_all(jnp.broadcast_to(block[None], (chips, ROWS, LANES)), group...  18.8 us
    all_to_all x1, blocking collectives, per_device(): lax.all_to_all(copies, group + ('side',), 0, 0, tiled=True)  11.2 us
    pallas_call x4, Pallas kernels, call(): pl.pallas_call(kernel, out_shape=tuple((jax.ShapeDtypeStruct(*out) for ou...  7.43 us
    ppermute x1, waiting for transfers between devices, per_device(): other = lax.ppermute(mine, 'side', swap)  0.83 us
  transfers between devices with their start and end apart: 2, of which 1 were waited for; matrix products, arithmetic and copies ran while one was open for 0% of the time, Pallas kernels for 5%

profile of v5, /device:TPU:0, one launch (start us, length us, event | category | flops | bytes accessed | tf_op | source)
XLA Modules:
  0.0 39.8 jit_solution(17718111330782437725)
XLA Ops:
  0.6 1.1 %pack.1 = (bf16[72,128]{1,0:T(8,128)(2,1)S(1)}, f32[8,256]{1,0:T(8,128)S(1)}) custom-call(bf16[2,256]{1,0:T(2,128)(2,1)} %points_hbm.1, s32[1,256]{1,0:T(1,128)} %bitcast.6, f32[1,256]{1,0:T(1,128)} %bitcast.7, f32[32,256]{1,0:T(8,128)} %dir_ref.5), custom_call_target="tpu_custom_call" | custom-call | tf_op jit(solution)/shard_map/pack/pallas_call | solution.py:274
  1.8 0.0 copy-start
  1.8 0.0 copy-start.1
  1.8 18.8 %all_to_all.10.all_ref = bf16[16,72,128]{2,1,0:T(8,128)(2,1)S(1)} all-to-all(bf16[16,72,128]{2,1,0:T(8,128)(2,1)S(1)} %broadcast_in_dim.6), channel_id=1, replica_groups=mesh['row'=4,'pair'=4,'side'=2] {'row','pair'}, dimensions={0} | all-to-all | bytes 589824 | tf_op jit(solution)/shard_map/all_to_all | solution.py:301
  20.6 0.0 collective-permute-start
  20.6 0.0 copy-done
  20.6 0.0 copy-done.1
  20.7 1.9 %near_half.1 = (f32[32,256]{1,0:T(8,128)S(1)}, f32[40,256]{1,0:T(8,128)S(1)}, f32[32,128]{1,0:T(8,128)S(1)}, bf16[256,40]{1,0:T(8,128)(2,1)S(1)}) custom-call(f32[8,256]{1,0:T(8,128)S(1)} %get-tuple-element.11.own_ref, f32[32,256]{1,0:T(8,128)S(1)} %copy-done, f32[32,256]{1,0:T(8,128)S(1)} %copy-done.1, bf16[16,72,128]{2,1,0:T(8,128)(2,1)S(1)} %all_to_all.10.all_ref), custom_call_target="tpu_custom_call" | custom-call | tf_op jit(solution)/shard_map/near_half/pallas_call | solution.py:274
  22.5 0.0 collective-permute-done.all_ref
  22.5 1.9 %far_half.1 = (f32[32,256]{1,0:T(8,128)S(1)}, f32[6,4,128]{2,1,0:T(4,128)S(1)}) custom-call(f32[8,256]{1,0:T(8,128)S(1)} %get-tuple-element.11.own_ref, f32[32,256]{1,0:T(8,128)S(1)} %copy-done, f32[32,256]{1,0:T(8,128)S(1)} %copy-done.1, f32[32,128]{1,0:T(8,128)S(1)} %get-tuple-element.13.norm_ref, f32[32,256]{1,0:T(8,128)S(1)} %get-tuple-element.14.product_ref, ...), custom_call_target="tpu_custom_call" | custom-call | tf_op jit(solution)/shard_map/far_half/pallas_call | solution.py:274
  24.5 11.2 %all_to_all.11 = f32[32,3,4,128]{3,2,1,0:T(4,128)S(1)} all-to-all(f32[32,3,4,128]{3,2,1,0:T(4,128)S(1)} %bitcast.5), channel_id=1, replica_groups=mesh['row'=4,'pair'=4,'side'=2] {'row','pair','side'}, dimensions={0} | all-to-all | bytes 393216 | tf_op jit(solution)/shard_map/all_to_all | solution.py:316
  35.7 0.0 copy-start.2
  35.7 0.1 reduce_sum.9.mine_ref
  35.8 0.7 %collective-permute-start.1 = (f32[3,4,128]{2,1,0:T(4,128)S(1)}, f32[3,4,128]{2,1,0:T(4,128)S(1)}, u32[]{:S(2)}, u32[]{:S(2)}) collective-permute-start(f32[3,4,128]{2,1,0:T(4,128)S(1)} %reduce_sum.9.mine_ref), channel_id=1, source_target_pairs={{0,1},{1,0},{2,3},{3,2},{4,5},{5,4},{6,7},{7,6},{8,9},{9,8},{10,11... | collective-permute-start | bytes 18440 | tf_op jit(solution)/shard_map/ppermute | solution.py:317
  36.4 0.8 %collective-permute-done.1.other_ref = f32[3,4,128]{2,1,0:T(4,128)S(1)} collective-permute-done((f32[3,4,128]{2,1,0:T(4,128)S(1)}, f32[3,4,128]{2,1,0:T(4,128)S(1)}, u32[]{:S(2)}, u32[]{:S(2)}) %collective-permute-start.1) | collective-permute-done | bytes 6176 | tf_op jit(solution)/shard_map/ppermute | solution.py:317
  37.2 0.0 copy-done.2
  37.3 2.5 %final.1 = (f32[32,256]{1,0:T(8,128)}, f32[32,256]{1,0:T(8,128)}, f32[32,256]{1,0:T(8,128)}) custom-call(f32[3,4,128]{2,1,0:T(4,128)S(1)} %reduce_sum.9.mine_ref, f32[3,4,128]{2,1,0:T(4,128)S(1)} %collective-permute-done.1.other_ref, f32[32,256]{1,0:T(8,128)S(1)} %copy-done.2, f32[32,256]{1,0:T(8,128)S(1)} %copy-done.1, f32[32,256]{1,0:T(8,128)S(1)} %copy-done, ...), custom_call_target="tpu_custom_call" | custom-call | tf_op jit(solution)/shard_map/final/pallas_call | solution.py:274
  (2 shorter events, 0.1 us)
Async XLA Ops:
  1.8 18.8 %copy-start = (f32[32,256]{1,0:T(8,128)S(1)}, f32[32,256]{1,0:T(8,128)}, u32[]{:S(2)}) copy-start(f32[32,256]{1,0:T(8,128)} %dir_ref.5) | copy-start | bytes 98308
  1.8 18.8 %copy-start.1 = (f32[32,256]{1,0:T(8,128)S(1)}, f32[32,256]{1,0:T(8,128)}, u32[]{:S(2)}) copy-start(f32[32,256]{1,0:T(8,128)} %res_ref.5) | copy-start | bytes 98308
  20.6 1.9 %collective-permute-start = (bf16[16,72,128]{2,1,0:T(8,128)(2,1)S(1)}, bf16[16,72,128]{2,1,0:T(8,128)(2,1)S(1)}, u32[]{:S(2)}, u32[]{:S(2)}) collective-permute-start(bf16[16,72,128]{2,1,0:T(8,128)(2,1)S(1)} %all_to_all.10.all_ref), channel_id=1, source_target_pairs={{0,1},{1,0},{2,3},{3,2},{4,5},{5,4},{6,7},{7,6},{8,9},{9,8},{10,11... | collective-permute-start | bytes 884744 | tf_op jit(solution)/shard_map/ppermute | solution.py:302
  35.7 1.5 %copy-start.2 = (f32[32,256]{1,0:T(8,128)S(1)}, f32[32,256]{1,0:T(8,128)}, u32[]{:S(2)}) copy-start(f32[32,256]{1,0:T(8,128)} %sol_ref.1) | copy-start | bytes 98308
  35.8 1.5 %collective-permute-start.1 = (f32[3,4,128]{2,1,0:T(4,128)S(1)}, f32[3,4,128]{2,1,0:T(4,128)S(1)}, u32[]{:S(2)}, u32[]{:S(2)}) collective-permute-start(f32[3,4,128]{2,1,0:T(4,128)S(1)} %reduce_sum.9.mine_ref), channel_id=1, source_target_pairs={{0,1},{1,0},{2,3},{3,2},{4,5},{5,4},{6,7},{7,6},{8,9},{9,8},{10,11... | collective-permute-start | bytes 18440 | tf_op jit(solution)/shard_map/ppermute | solution.py:317

commit v6 on v5

--- a/solution.py
+++ b/solution.py
@@ -223,24 +223,30 @@
     return first, second
 
 
+def solve_pair(a, b, c, d):
+    inverse = 1.0 / a
+    lower = c * inverse
+    inverse_rest = 1.0 / (d - lower * b)
+
+    def solve(top, bottom):
+        second = (bottom - lower * top) * inverse_rest
+        return (top - b * second) * inverse, second
+
+    return solve
+
+
 def eliminate(work, step):
     rows = lax.broadcasted_iota(jnp.int32, work.shape, 0)
     cols = [jnp.broadcast_to(work[:, step + n : step + n + 1], work.shape) for n in range(4)]
     line = [work[step + n : step + n + 1, :] for n in range(4)]
     piv = [[cols[m][step + n : step + n + 1, :] for m in range(4)] for n in range(4)]
-    inverse = 1.0 / (piv[0][0] * piv[1][1] - piv[0][1] * piv[1][0])
-
-    def first_block(top, bottom):
-        return (piv[1][1] * top - piv[0][1] * bottom) * inverse, (piv[0][0] * bottom - piv[1][0] * top) * inverse
-
+    first_block = solve_pair(piv[0][0], piv[0][1], piv[1][0], piv[1][1])
     new0, new1 = first_block(line[0], line[1])
     cross = [first_block(piv[0][m], piv[1][m]) for m in (2, 3)]
     rest = [[piv[n][m + 2] - piv[n][0] * cross[m][0] - piv[n][1] * cross[m][1] for m in range(2)] for n in (2, 3)]
-    inverse_rest = 1.0 / (rest[0][0] * rest[1][1] - rest[0][1] * rest[1][0])
     left2 = line[2] - piv[2][0] * new0 - piv[2][1] * new1
     left3 = line[3] - piv[3][0] * new0 - piv[3][1] * new1
-    new2 = (rest[1][1] * left2 - rest[0][1] * left3) * inverse_rest
-    new3 = (rest[0][0] * left3 - rest[1][0] * left2) * inverse_rest
+    new2, new3 = solve_pair(rest[0][0], rest[0][1], rest[1][0], rest[1][1])(left2, left3)
     new0 = new0 - cross[0][0] * new2 - cross[1][0] * new3
     new1 = new1 - cross[0][1] * new2 - cross[1][1] * new3
     work = work - (cols[0] * new0 + cols[1] * new1) - (cols[2] * new2 + cols[3] * new3)

time: 40 us -> 40.3 us (level)
  no operation moved by 1% of the time
where the time goes in v6:
time: 40.3 us; the launch traced here: 40 us
  blocking collectives  30 us (74%)
  Pallas kernels  7.68 us (19%)
  waiting for transfers between devices  0.83 us (2%)
  between operations  0.69 us (2%)
  starting transfers between devices  0.66 us (2%)
    all_to_all x1, blocking collectives, per_device(): lax.all_to_all(jnp.broadcast_to(block[None], (chips, ROWS, LANES)), group...  18.8 us
    all_to_all x1, blocking collectives, per_device(): lax.all_to_all(copies, group + ('side',), 0, 0, tiled=True)  11.2 us
    pallas_call x4, Pallas kernels, call(): pl.pallas_call(kernel, out_shape=tuple((jax.ShapeDtypeStruct(*out) for ou...  7.68 us
    ppermute x1, waiting for transfers between devices, per_device(): other = lax.ppermute(mine, 'side', swap)  0.83 us
  transfers between devices with their start and end apart: 2, of which 1 were waited for; matrix products, arithmetic and copies ran while one was open for 0% of the time, Pallas kernels for 5%

profile of v6, /device:TPU:0, one launch (start us, length us, event | category | flops | bytes accessed | tf_op | source)
XLA Modules:
  0.0 40.0 jit_solution(9238640662921253908)
XLA Ops:
  0.6 1.1 %pack.1 = (bf16[72,128]{1,0:T(8,128)(2,1)S(1)}, f32[8,256]{1,0:T(8,128)S(1)}) custom-call(bf16[2,256]{1,0:T(2,128)(2,1)} %points_hbm.1, s32[1,256]{1,0:T(1,128)} %bitcast.6, f32[1,256]{1,0:T(1,128)} %bitcast.7, f32[32,256]{1,0:T(8,128)} %dir_ref.5), custom_call_target="tpu_custom_call" | custom-call | tf_op jit(solution)/shard_map/pack/pallas_call | solution.py:280
  1.8 0.0 copy-start
  1.8 0.0 copy-start.1
  1.8 18.8 %all_to_all.10.all_ref = bf16[16,72,128]{2,1,0:T(8,128)(2,1)S(1)} all-to-all(bf16[16,72,128]{2,1,0:T(8,128)(2,1)S(1)} %broadcast_in_dim.6), channel_id=1, replica_groups=mesh['row'=4,'pair'=4,'side'=2] {'row','pair'}, dimensions={0} | all-to-all | bytes 589824 | tf_op jit(solution)/shard_map/all_to_all | solution.py:307
  20.6 0.0 collective-permute-start
  20.6 0.0 copy-done
  20.6 0.0 copy-done.1
  20.7 1.9 %near_half.1 = (f32[32,256]{1,0:T(8,128)S(1)}, f32[40,256]{1,0:T(8,128)S(1)}, f32[32,128]{1,0:T(8,128)S(1)}, bf16[256,40]{1,0:T(8,128)(2,1)S(1)}) custom-call(f32[8,256]{1,0:T(8,128)S(1)} %get-tuple-element.11.own_ref, f32[32,256]{1,0:T(8,128)S(1)} %copy-done, f32[32,256]{1,0:T(8,128)S(1)} %copy-done.1, bf16[16,72,128]{2,1,0:T(8,128)(2,1)S(1)} %all_to_all.10.all_ref), custom_call_target="tpu_custom_call" | custom-call | tf_op jit(solution)/shard_map/near_half/pallas_call | solution.py:280
  22.5 0.0 collective-permute-done.all_ref
  22.5 1.9 %far_half.1 = (f32[32,256]{1,0:T(8,128)S(1)}, f32[6,4,128]{2,1,0:T(4,128)S(1)}) custom-call(f32[8,256]{1,0:T(8,128)S(1)} %get-tuple-element.11.own_ref, f32[32,256]{1,0:T(8,128)S(1)} %copy-done, f32[32,256]{1,0:T(8,128)S(1)} %copy-done.1, f32[32,128]{1,0:T(8,128)S(1)} %get-tuple-element.13.norm_ref, f32[32,256]{1,0:T(8,128)S(1)} %get-tuple-element.14.product_ref, ...), custom_call_target="tpu_custom_call" | custom-call | tf_op jit(solution)/shard_map/far_half/pallas_call | solution.py:280
  24.5 11.2 %all_to_all.11 = f32[32,3,4,128]{3,2,1,0:T(4,128)S(1)} all-to-all(f32[32,3,4,128]{3,2,1,0:T(4,128)S(1)} %bitcast.5), channel_id=1, replica_groups=mesh['row'=4,'pair'=4,'side'=2] {'row','pair','side'}, dimensions={0} | all-to-all | bytes 393216 | tf_op jit(solution)/shard_map/all_to_all | solution.py:322
  35.7 0.0 copy-start.2
  35.7 0.1 reduce_sum.9.mine_ref
  35.8 0.7 %collective-permute-start.1 = (f32[3,4,128]{2,1,0:T(4,128)S(1)}, f32[3,4,128]{2,1,0:T(4,128)S(1)}, u32[]{:S(2)}, u32[]{:S(2)}) collective-permute-start(f32[3,4,128]{2,1,0:T(4,128)S(1)} %reduce_sum.9.mine_ref), channel_id=1, source_target_pairs={{0,1},{1,0},{2,3},{3,2},{4,5},{5,4},{6,7},{7,6},{8,9},{9,8},{10,11... | collective-permute-start | bytes 18440 | tf_op jit(solution)/shard_map/ppermute | solution.py:323
  36.4 0.8 %collective-permute-done.1.other_ref = f32[3,4,128]{2,1,0:T(4,128)S(1)} collective-permute-done((f32[3,4,128]{2,1,0:T(4,128)S(1)}, f32[3,4,128]{2,1,0:T(4,128)S(1)}, u32[]{:S(2)}, u32[]{:S(2)}) %collective-permute-start.1) | collective-permute-done | bytes 6176 | tf_op jit(solution)/shard_map/ppermute | solution.py:323
  37.2 0.0 copy-done.2
  37.3 2.7 %final.1 = (f32[32,256]{1,0:T(8,128)}, f32[32,256]{1,0:T(8,128)}, f32[32,256]{1,0:T(8,128)}) custom-call(f32[3,4,128]{2,1,0:T(4,128)S(1)} %reduce_sum.9.mine_ref, f32[3,4,128]{2,1,0:T(4,128)S(1)} %collective-permute-done.1.other_ref, f32[32,256]{1,0:T(8,128)S(1)} %copy-done.2, f32[32,256]{1,0:T(8,128)S(1)} %copy-done.1, f32[32,256]{1,0:T(8,128)S(1)} %copy-done, ...), custom_call_target="tpu_custom_call" | custom-call | tf_op jit(solution)/shard_map/final/pallas_call | solution.py:280
  (2 shorter events, 0.1 us)
Async XLA Ops:
  1.8 18.8 %copy-start = (f32[32,256]{1,0:T(8,128)S(1)}, f32[32,256]{1,0:T(8,128)}, u32[]{:S(2)}) copy-start(f32[32,256]{1,0:T(8,128)} %dir_ref.5) | copy-start | bytes 98308
  1.8 18.8 %copy-start.1 = (f32[32,256]{1,0:T(8,128)S(1)}, f32[32,256]{1,0:T(8,128)}, u32[]{:S(2)}) copy-start(f32[32,256]{1,0:T(8,128)} %res_ref.5) | copy-start | bytes 98308
  20.6 1.9 %collective-permute-start = (bf16[16,72,128]{2,1,0:T(8,128)(2,1)S(1)}, bf16[16,72,128]{2,1,0:T(8,128)(2,1)S(1)}, u32[]{:S(2)}, u32[]{:S(2)}) collective-permute-start(bf16[16,72,128]{2,1,0:T(8,128)(2,1)S(1)} %all_to_all.10.all_ref), channel_id=1, source_target_pairs={{0,1},{1,0},{2,3},{3,2},{4,5},{5,4},{6,7},{7,6},{8,9},{9,8},{10,11... | collective-permute-start | bytes 884744 | tf_op jit(solution)/shard_map/ppermute | solution.py:308
  35.7 1.5 %copy-start.2 = (f32[32,256]{1,0:T(8,128)S(1)}, f32[32,256]{1,0:T(8,128)}, u32[]{:S(2)}) copy-start(f32[32,256]{1,0:T(8,128)} %sol_ref.1) | copy-start | bytes 98308
  35.8 1.5 %collective-permute-start.1 = (f32[3,4,128]{2,1,0:T(4,128)S(1)}, f32[3,4,128]{2,1,0:T(4,128)S(1)}, u32[]{:S(2)}, u32[]{:S(2)}) collective-permute-start(f32[3,4,128]{2,1,0:T(4,128)S(1)} %reduce_sum.9.mine_ref), channel_id=1, source_target_pairs={{0,1},{1,0},{2,3},{3,2},{4,5},{5,4},{6,7},{7,6},{8,9},{9,8},{10,11... | collective-permute-start | bytes 18440 | tf_op jit(solution)/shard_map/ppermute | solution.py:323

commit v7 on v6

--- a/solution.py
+++ b/solution.py
@@ -43,25 +43,26 @@
 def pack_kernel(
     points_hbm, dist_hbm, noise_hbm, dir_hbm, pack_ref, own_ref, points_ref, dist_ref, noise_ref, dir_ref, sems
 ):
-    pairs = ((points_hbm, points_ref), (dist_hbm, dist_ref), (noise_hbm, noise_ref), (dir_hbm, dir_ref))
+    pairs = ((dir_hbm, dir_ref), (dist_hbm, dist_ref), (points_hbm, points_ref), (noise_hbm, noise_ref))
     copies = [pltpu.make_async_copy(src, dst, sems.at[n]) for n, (src, dst) in enumerate(pairs)]
     for copy in copies:
         copy.start()
-    for copy in copies:
-        copy.wait()
     rhs, count = dir_ref.shape
+    copies[1].wait()
     dist = dist_ref[...]
-    pts = points_ref[...].astype(F32)
-    own_ref[...] = jnp.concatenate(
-        [pts, dist.astype(F32), noise_ref[...], jnp.zeros((4, count), F32)], axis=0
-    )
-    high, mid, low = three_pieces(dir_ref[...])
     first = dist[:, 0:1]
     last = dist[:, count - 1 : count]
     row = lax.broadcasted_iota(jnp.int32, (8, count), 0)
     picked = jnp.where(row == 0, first, last)
     wanted = (row == 0) | ((row == 1) & (first != last))
     mask = (wanted & (dist == picked)).astype(F32).astype(BF16)
+    for copy in (copies[0], copies[2], copies[3]):
+        copy.wait()
+    pts = points_ref[...].astype(F32)
+    own_ref[...] = jnp.concatenate(
+        [pts, dist.astype(F32), noise_ref[...], jnp.zeros((4, count), F32)], axis=0
+    )
+    high, mid, low = three_pieces(dir_ref[...])
     ones = jnp.ones((LANES - 3 * rhs, count), BF16)
     edge = dot_bf16(mask, jnp.concatenate([high, high, high, ones], axis=0), ((1,), (1,)))
     edge = edge + dot_bf16(mask, jnp.concatenate([mid, mid, mid, 0 * ones], axis=0), ((1,), (1,)))
@@ -213,14 +214,13 @@
             rows = jnp.where(group8 == source, moved, rows)
         parts.append(rows)
     flat = jnp.concatenate(parts, axis=0)
-    turned = flat.T
-    turned = jnp.concatenate([turned[0:32], turned[32:64], turned[64:96], turned[96:128]], axis=1)
     row, col, group = lane_groups(32)
+    spread = jnp.concatenate([jnp.where(group == n, flat, 0.0) for n in range(4)], axis=0).T
+    turned = (spread[0:32] + spread[32:64]) + (spread[64:96] + spread[96:128])
     diag = jnp.where(col[0:1] == 0, pltpu.roll(flat[0:8], 62, 1)[1:2], pltpu.roll(flat[0:8], 64, 1)[0:1])
     direct = (group == 2) | ((group <= 1) & (col <= row)) | ((group == 3) & (col > row))
     first = jnp.where(direct, flat, jnp.where((group == 3) & (col == row), diag, turned))
-    second = pltpu.roll(jnp.where(group == 1, first, turned), 96, 1)
-    return first, second
+    return first, jnp.where(group == 1, first, turned)
 
 
 def solve_pair(a, b, c, d):
@@ -235,9 +235,9 @@
     return solve
 
 
-def eliminate(work, step):
+def eliminate(work, step, at):
     rows = lax.broadcasted_iota(jnp.int32, work.shape, 0)
-    cols = [jnp.broadcast_to(work[:, step + n : step + n + 1], work.shape) for n in range(4)]
+    cols = [jnp.broadcast_to(work[:, at + step + n : at + step + n + 1], work.shape) for n in range(4)]
     line = [work[step + n : step + n + 1, :] for n in range(4)]
     piv = [[cols[m][step + n : step + n + 1, :] for m in range(4)] for n in range(4)]
     first_block = solve_pair(piv[0][0], piv[0][1], piv[1][0], piv[1][1])
@@ -262,13 +262,13 @@
     quarters += [jnp.where(even, other_ref[n], mine_ref[n]) for n in range(3)]
     first, second = unpack_gram([jnp.concatenate(quarters[2 * n : 2 * n + 2], axis=0) for n in range(3)])
     for step in range(0, rhs, 4):
-        first = eliminate(first, step)
-        second = eliminate(second, step)
+        first = eliminate(first, step, 0)
+        second = eliminate(second, step, rhs)
     alpha = first[:, 32:64]
     row = lax.broadcasted_iota(jnp.int32, (rhs, rhs), 0)
     col = lax.broadcasted_iota(jnp.int32, (rhs, rhs), 1)
     eye = (row == col).astype(F32)
-    beta = eye - first[:, 64:96] + dot_f32(first[:, 96:128] - second[:, 32:64], alpha, ((1,), (0,)))
+    beta = eye - first[:, 64:96] + dot_f32(first[:, 96:128] - second[:, 64:96], alpha, ((1,), (0,)))
     direction = dir_ref[...]
     new_sol_ref[...] = sol_ref[...] + dot_f32(alpha, direction, ((0,), (0,)))
     new_res = res_ref[...] - dot_f32(alpha, image_ref[...], ((0,), (0,)))

time: 40.3 us -> 40.1 us (level)
  no operation moved by 1% of the time
where the time goes in v7:
time: 40.1 us; the launch traced here: 39.8 us
  blocking collectives  30 us (75%)
  Pallas kernels  7.46 us (19%)
  waiting for transfers between devices  0.83 us (2%)
  between operations  0.69 us (2%)
  starting transfers between devices  0.66 us (2%)
    all_to_all x1, blocking collectives, per_device(): lax.all_to_all(jnp.broadcast_to(block[None], (chips, ROWS, LANES)), group...  18.8 us
    all_to_all x1, blocking collectives, per_device(): lax.all_to_all(copies, group + ('side',), 0, 0, tiled=True)  11.2 us
    pallas_call x4, Pallas kernels, call(): pl.pallas_call(kernel, out_shape=tuple((jax.ShapeDtypeStruct(*out) for ou...  7.46 us
    ppermute x1, waiting for transfers between devices, per_device(): other = lax.ppermute(mine, 'side', swap)  0.83 us
  transfers between devices with their start and end apart: 2, of which 1 were waited for; matrix products, arithmetic and copies ran while one was open for 0% of the time, Pallas kernels for 5%

profile of v7, /device:TPU:0, one launch (start us, length us, event | category | flops | bytes accessed | tf_op | source)
XLA Modules:
  0.0 39.8 jit_solution(18018319838003133011)
XLA Ops:
  0.6 1.1 %pack.1 = (bf16[72,128]{1,0:T(8,128)(2,1)S(1)}, f32[8,256]{1,0:T(8,128)S(1)}) custom-call(bf16[2,256]{1,0:T(2,128)(2,1)} %points_hbm.1, s32[1,256]{1,0:T(1,128)} %bitcast.6, f32[1,256]{1,0:T(1,128)} %bitcast.7, f32[32,256]{1,0:T(8,128)} %dir_ref.5), custom_call_target="tpu_custom_call" | custom-call | tf_op jit(solution)/shard_map/pack/pallas_call | solution.py:280
  1.8 0.0 copy-start
  1.8 0.0 copy-start.1
  1.8 18.8 %all_to_all.10.all_ref = bf16[16,72,128]{2,1,0:T(8,128)(2,1)S(1)} all-to-all(bf16[16,72,128]{2,1,0:T(8,128)(2,1)S(1)} %broadcast_in_dim.6), channel_id=1, replica_groups=mesh['row'=4,'pair'=4,'side'=2] {'row','pair'}, dimensions={0} | all-to-all | bytes 589824 | tf_op jit(solution)/shard_map/all_to_all | solution.py:307
  20.6 0.0 collective-permute-start
  20.6 0.0 copy-done
  20.6 0.0 copy-done.1
  20.6 1.9 %near_half.1 = (f32[32,256]{1,0:T(8,128)S(1)}, f32[40,256]{1,0:T(8,128)S(1)}, f32[32,128]{1,0:T(8,128)S(1)}, bf16[256,40]{1,0:T(8,128)(2,1)S(1)}) custom-call(f32[8,256]{1,0:T(8,128)S(1)} %get-tuple-element.11.own_ref, f32[32,256]{1,0:T(8,128)S(1)} %copy-done, f32[32,256]{1,0:T(8,128)S(1)} %copy-done.1, bf16[16,72,128]{2,1,0:T(8,128)(2,1)S(1)} %all_to_all.10.all_ref), custom_call_target="tpu_custom_call" | custom-call | tf_op jit(solution)/shard_map/near_half/pallas_call | solution.py:280
  22.5 0.0 collective-permute-done.all_ref
  22.5 1.9 %far_half.1 = (f32[32,256]{1,0:T(8,128)S(1)}, f32[6,4,128]{2,1,0:T(4,128)S(1)}) custom-call(f32[8,256]{1,0:T(8,128)S(1)} %get-tuple-element.11.own_ref, f32[32,256]{1,0:T(8,128)S(1)} %copy-done, f32[32,256]{1,0:T(8,128)S(1)} %copy-done.1, f32[32,128]{1,0:T(8,128)S(1)} %get-tuple-element.13.norm_ref, f32[32,256]{1,0:T(8,128)S(1)} %get-tuple-element.14.product_ref, ...), custom_call_target="tpu_custom_call" | custom-call | tf_op jit(solution)/shard_map/far_half/pallas_call | solution.py:280
  24.4 11.2 %all_to_all.11 = f32[32,3,4,128]{3,2,1,0:T(4,128)S(1)} all-to-all(f32[32,3,4,128]{3,2,1,0:T(4,128)S(1)} %bitcast.5), channel_id=1, replica_groups=mesh['row'=4,'pair'=4,'side'=2] {'row','pair','side'}, dimensions={0} | all-to-all | bytes 393216 | tf_op jit(solution)/shard_map/all_to_all | solution.py:322
  35.6 0.0 copy-start.2
  35.6 0.1 reduce_sum.9.mine_ref
  35.7 0.7 %collective-permute-start.1 = (f32[3,4,128]{2,1,0:T(4,128)S(1)}, f32[3,4,128]{2,1,0:T(4,128)S(1)}, u32[]{:S(2)}, u32[]{:S(2)}) collective-permute-start(f32[3,4,128]{2,1,0:T(4,128)S(1)} %reduce_sum.9.mine_ref), channel_id=1, source_target_pairs={{0,1},{1,0},{2,3},{3,2},{4,5},{5,4},{6,7},{7,6},{8,9},{9,8},{10,11... | collective-permute-start | bytes 18440 | tf_op jit(solution)/shard_map/ppermute | solution.py:323
  36.4 0.8 %collective-permute-done.1.other_ref = f32[3,4,128]{2,1,0:T(4,128)S(1)} collective-permute-done((f32[3,4,128]{2,1,0:T(4,128)S(1)}, f32[3,4,128]{2,1,0:T(4,128)S(1)}, u32[]{:S(2)}, u32[]{:S(2)}) %collective-permute-start.1) | collective-permute-done | bytes 6176 | tf_op jit(solution)/shard_map/ppermute | solution.py:323
  37.2 0.0 copy-done.2
  37.2 2.6 %final.1 = (f32[32,256]{1,0:T(8,128)}, f32[32,256]{1,0:T(8,128)}, f32[32,256]{1,0:T(8,128)}) custom-call(f32[3,4,128]{2,1,0:T(4,128)S(1)} %reduce_sum.9.mine_ref, f32[3,4,128]{2,1,0:T(4,128)S(1)} %collective-permute-done.1.other_ref, f32[32,256]{1,0:T(8,128)S(1)} %copy-done.2, f32[32,256]{1,0:T(8,128)S(1)} %copy-done.1, f32[32,256]{1,0:T(8,128)S(1)} %copy-done, ...), custom_call_target="tpu_custom_call" | custom-call | tf_op jit(solution)/shard_map/final/pallas_call | solution.py:280
  (2 shorter events, 0.1 us)
Async XLA Ops:
  1.8 18.8 %copy-start = (f32[32,256]{1,0:T(8,128)S(1)}, f32[32,256]{1,0:T(8,128)}, u32[]{:S(2)}) copy-start(f32[32,256]{1,0:T(8,128)} %dir_ref.5) | copy-start | bytes 98308
  1.8 18.8 %copy-start.1 = (f32[32,256]{1,0:T(8,128)S(1)}, f32[32,256]{1,0:T(8,128)}, u32[]{:S(2)}) copy-start(f32[32,256]{1,0:T(8,128)} %res_ref.5) | copy-start | bytes 98308
  20.6 1.9 %collective-permute-start = (bf16[16,72,128]{2,1,0:T(8,128)(2,1)S(1)}, bf16[16,72,128]{2,1,0:T(8,128)(2,1)S(1)}, u32[]{:S(2)}, u32[]{:S(2)}) collective-permute-start(bf16[16,72,128]{2,1,0:T(8,128)(2,1)S(1)} %all_to_all.10.all_ref), channel_id=1, source_target_pairs={{0,1},{1,0},{2,3},{3,2},{4,5},{5,4},{6,7},{7,6},{8,9},{9,8},{10,11... | collective-permute-start | bytes 884744 | tf_op jit(solution)/shard_map/ppermute | solution.py:308
  35.6 1.5 %copy-start.2 = (f32[32,256]{1,0:T(8,128)S(1)}, f32[32,256]{1,0:T(8,128)}, u32[]{:S(2)}) copy-start(f32[32,256]{1,0:T(8,128)} %sol_ref.1) | copy-start | bytes 98308
  35.7 1.5 %collective-permute-start.1 = (f32[3,4,128]{2,1,0:T(4,128)S(1)}, f32[3,4,128]{2,1,0:T(4,128)S(1)}, u32[]{:S(2)}, u32[]{:S(2)}) collective-permute-start(f32[3,4,128]{2,1,0:T(4,128)S(1)} %reduce_sum.9.mine_ref), channel_id=1, source_target_pairs={{0,1},{1,0},{2,3},{3,2},{4,5},{5,4},{6,7},{7,6},{8,9},{9,8},{10,11... | collective-permute-start | bytes 18440 | tf_op jit(solution)/shard_map/ppermute | solution.py:323

commit v8 on v7

--- a/solution.py
+++ b/solution.py
@@ -255,6 +255,16 @@
     return work
 
 
+def spread_left(vals):
+    high, mid, low = (piece.astype(F32) for piece in three_pieces(vals))
+    return jnp.concatenate([high, high, mid, high, mid, low], axis=0).astype(BF16)
+
+
+def spread_right(vals):
+    high, mid, low = three_pieces(vals)
+    return jnp.concatenate([high, mid, high, low, mid, high], axis=0)
+
+
 def final_kernel(mine_ref, other_ref, sol_ref, res_ref, dir_ref, image_ref, new_sol_ref, new_res_ref, new_dir_ref):
     rhs = sol_ref.shape[0]
     even = lax.axis_index("side") == 0
@@ -269,11 +279,12 @@
     col = lax.broadcasted_iota(jnp.int32, (rhs, rhs), 1)
     eye = (row == col).astype(F32)
     beta = eye - first[:, 64:96] + dot_f32(first[:, 96:128] - second[:, 64:96], alpha, ((1,), (0,)))
-    direction = dir_ref[...]
-    new_sol_ref[...] = sol_ref[...] + dot_f32(alpha, direction, ((0,), (0,)))
-    new_res = res_ref[...] - dot_f32(alpha, image_ref[...], ((0,), (0,)))
+    direction, image = spread_right(dir_ref[...]), spread_right(image_ref[...])
+    spread_alpha = spread_left(alpha)
+    new_sol_ref[...] = sol_ref[...] + dot_bf16(spread_alpha, direction, ((0,), (0,)))
+    new_res = res_ref[...] - dot_bf16(spread_alpha, image, ((0,), (0,)))
     new_res_ref[...] = new_res
-    new_dir_ref[...] = new_res + dot_f32(beta, direction, ((0,), (0,)))
+    new_dir_ref[...] = new_res + dot_bf16(spread_left(beta), direction, ((0,), (0,)))
 
 
 def call(kernel, outs, ins, name, megabytes, scratch=(), space=pltpu.VMEM):

time: 40.1 us -> 40 us (level)
  no operation moved by 1% of the time
where the time goes in v8:
time: 40 us; the launch traced here: 39.7 us
  blocking collectives  30 us (75%)
  Pallas kernels  7.41 us (19%)
  waiting for transfers between devices  0.83 us (2%)
  between operations  0.69 us (2%)
  starting transfers between devices  0.66 us (2%)
    all_to_all x1, blocking collectives, per_device(): lax.all_to_all(jnp.broadcast_to(block[None], (chips, ROWS, LANES)), group...  18.8 us
    all_to_all x1, blocking collectives, per_device(): lax.all_to_all(copies, group + ('side',), 0, 0, tiled=True)  11.2 us
    pallas_call x4, Pallas kernels, call(): pl.pallas_call(kernel, out_shape=tuple((jax.ShapeDtypeStruct(*out) for ou...  7.41 us
    ppermute x1, waiting for transfers between devices, per_device(): other = lax.ppermute(mine, 'side', swap)  0.83 us
  transfers between devices with their start and end apart: 2, of which 1 were waited for; matrix products, arithmetic and copies ran while one was open for 0% of the time, Pallas kernels for 5%

profile of v8, /device:TPU:0, one launch (start us, length us, event | category | flops | bytes accessed | tf_op | source)
XLA Modules:
  0.0 39.7 jit_solution(8015471303613292258)
XLA Ops:
  0.6 1.1 %pack.1 = (bf16[72,128]{1,0:T(8,128)(2,1)S(1)}, f32[8,256]{1,0:T(8,128)S(1)}) custom-call(bf16[2,256]{1,0:T(2,128)(2,1)} %points_hbm.1, s32[1,256]{1,0:T(1,128)} %bitcast.6, f32[1,256]{1,0:T(1,128)} %bitcast.7, f32[32,256]{1,0:T(8,128)} %dir_ref.5), custom_call_target="tpu_custom_call" | custom-call | tf_op jit(solution)/shard_map/pack/pallas_call | solution.py:291
  1.8 0.0 copy-start
  1.8 0.0 copy-start.1
  1.8 18.8 %all_to_all.10.all_ref = bf16[16,72,128]{2,1,0:T(8,128)(2,1)S(1)} all-to-all(bf16[16,72,128]{2,1,0:T(8,128)(2,1)S(1)} %broadcast_in_dim.6), channel_id=1, replica_groups=mesh['row'=4,'pair'=4,'side'=2] {'row','pair'}, dimensions={0} | all-to-all | bytes 589824 | tf_op jit(solution)/shard_map/all_to_all | solution.py:318
  20.6 0.0 collective-permute-start
  20.6 0.0 copy-done
  20.6 0.0 copy-done.1
  20.6 1.9 %near_half.1 = (f32[32,256]{1,0:T(8,128)S(1)}, f32[40,256]{1,0:T(8,128)S(1)}, f32[32,128]{1,0:T(8,128)S(1)}, bf16[256,40]{1,0:T(8,128)(2,1)S(1)}) custom-call(f32[8,256]{1,0:T(8,128)S(1)} %get-tuple-element.11.own_ref, f32[32,256]{1,0:T(8,128)S(1)} %copy-done, f32[32,256]{1,0:T(8,128)S(1)} %copy-done.1, bf16[16,72,128]{2,1,0:T(8,128)(2,1)S(1)} %all_to_all.10.all_ref), custom_call_target="tpu_custom_call" | custom-call | tf_op jit(solution)/shard_map/near_half/pallas_call | solution.py:291
  22.5 0.0 collective-permute-done.all_ref
  22.5 1.9 %far_half.1 = (f32[32,256]{1,0:T(8,128)S(1)}, f32[6,4,128]{2,1,0:T(4,128)S(1)}) custom-call(f32[8,256]{1,0:T(8,128)S(1)} %get-tuple-element.11.own_ref, f32[32,256]{1,0:T(8,128)S(1)} %copy-done, f32[32,256]{1,0:T(8,128)S(1)} %copy-done.1, f32[32,128]{1,0:T(8,128)S(1)} %get-tuple-element.13.norm_ref, f32[32,256]{1,0:T(8,128)S(1)} %get-tuple-element.14.product_ref, ...), custom_call_target="tpu_custom_call" | custom-call | tf_op jit(solution)/shard_map/far_half/pallas_call | solution.py:291
  24.4 11.2 %all_to_all.11 = f32[32,3,4,128]{3,2,1,0:T(4,128)S(1)} all-to-all(f32[32,3,4,128]{3,2,1,0:T(4,128)S(1)} %bitcast.5), channel_id=1, replica_groups=mesh['row'=4,'pair'=4,'side'=2] {'row','pair','side'}, dimensions={0} | all-to-all | bytes 393216 | tf_op jit(solution)/shard_map/all_to_all | solution.py:333
  35.6 0.0 copy-start.2
  35.6 0.1 reduce_sum.9.mine_ref
  35.7 0.7 %collective-permute-start.1 = (f32[3,4,128]{2,1,0:T(4,128)S(1)}, f32[3,4,128]{2,1,0:T(4,128)S(1)}, u32[]{:S(2)}, u32[]{:S(2)}) collective-permute-start(f32[3,4,128]{2,1,0:T(4,128)S(1)} %reduce_sum.9.mine_ref), channel_id=1, source_target_pairs={{0,1},{1,0},{2,3},{3,2},{4,5},{5,4},{6,7},{7,6},{8,9},{9,8},{10,11... | collective-permute-start | bytes 18440 | tf_op jit(solution)/shard_map/ppermute | solution.py:334
  36.4 0.8 %collective-permute-done.1.other_ref = f32[3,4,128]{2,1,0:T(4,128)S(1)} collective-permute-done((f32[3,4,128]{2,1,0:T(4,128)S(1)}, f32[3,4,128]{2,1,0:T(4,128)S(1)}, u32[]{:S(2)}, u32[]{:S(2)}) %collective-permute-start.1) | collective-permute-done | bytes 6176 | tf_op jit(solution)/shard_map/ppermute | solution.py:334
  37.2 0.0 copy-done.2
  37.2 2.5 %final.1 = (f32[32,256]{1,0:T(8,128)}, f32[32,256]{1,0:T(8,128)}, f32[32,256]{1,0:T(8,128)}) custom-call(f32[3,4,128]{2,1,0:T(4,128)S(1)} %reduce_sum.9.mine_ref, f32[3,4,128]{2,1,0:T(4,128)S(1)} %collective-permute-done.1.other_ref, f32[32,256]{1,0:T(8,128)S(1)} %copy-done.2, f32[32,256]{1,0:T(8,128)S(1)} %copy-done.1, f32[32,256]{1,0:T(8,128)S(1)} %copy-done, ...), custom_call_target="tpu_custom_call" | custom-call | tf_op jit(solution)/shard_map/final/pallas_call | solution.py:291
  (2 shorter events, 0.1 us)
Async XLA Ops:
  1.8 18.8 %copy-start = (f32[32,256]{1,0:T(8,128)S(1)}, f32[32,256]{1,0:T(8,128)}, u32[]{:S(2)}) copy-start(f32[32,256]{1,0:T(8,128)} %dir_ref.5) | copy-start | bytes 98308
  1.8 18.8 %copy-start.1 = (f32[32,256]{1,0:T(8,128)S(1)}, f32[32,256]{1,0:T(8,128)}, u32[]{:S(2)}) copy-start(f32[32,256]{1,0:T(8,128)} %res_ref.5) | copy-start | bytes 98308
  20.6 1.9 %collective-permute-start = (bf16[16,72,128]{2,1,0:T(8,128)(2,1)S(1)}, bf16[16,72,128]{2,1,0:T(8,128)(2,1)S(1)}, u32[]{:S(2)}, u32[]{:S(2)}) collective-permute-start(bf16[16,72,128]{2,1,0:T(8,128)(2,1)S(1)} %all_to_all.10.all_ref), channel_id=1, source_target_pairs={{0,1},{1,0},{2,3},{3,2},{4,5},{5,4},{6,7},{7,6},{8,9},{9,8},{10,11... | collective-permute-start | bytes 884744 | tf_op jit(solution)/shard_map/ppermute | solution.py:319
  35.6 1.5 %copy-start.2 = (f32[32,256]{1,0:T(8,128)S(1)}, f32[32,256]{1,0:T(8,128)}, u32[]{:S(2)}) copy-start(f32[32,256]{1,0:T(8,128)} %sol_ref.1) | copy-start | bytes 98308
  35.7 1.5 %collective-permute-start.1 = (f32[3,4,128]{2,1,0:T(4,128)S(1)}, f32[3,4,128]{2,1,0:T(4,128)S(1)}, u32[]{:S(2)}, u32[]{:S(2)}) collective-permute-start(f32[3,4,128]{2,1,0:T(4,128)S(1)} %reduce_sum.9.mine_ref), channel_id=1, source_target_pairs={{0,1},{1,0},{2,3},{3,2},{4,5},{5,4},{6,7},{7,6},{8,9},{9,8},{10,11... | collective-permute-start | bytes 18440 | tf_op jit(solution)/shard_map/ppermute | solution.py:334

commit v9 on v7

--- a/solution.py
+++ b/solution.py
@@ -140,10 +140,15 @@
     return product, extra, sums[3 * rhs + 1 : 3 * rhs + 2]
 
 
+def place_in_group(chips):
+    place = lax.axis_index(("row", "pair"))
+    return jnp.where(lax.axis_index("side") == 0, place, (place + chips // 2) % chips)
+
+
 def first_kernel(own_ref, dir_ref, res_ref, all_ref, product_ref, sums_ref, norm_ref, side_ref):
     rhs, count = dir_ref.shape
     side_ref[...] = own_side(own_ref[...]).T.astype(BF16)
-    product, extra, number = half_product(lax.axis_index(("row", "pair")), own_ref, all_ref, side_ref)
+    product, extra, number = half_product(place_in_group(all_ref.shape[0]), own_ref, all_ref, side_ref)
     product_ref[...] = product
     labels = lax.broadcasted_iota(jnp.int32, (64, count), 0).astype(F32)
     onehot = (labels == own_ref[2:3, :]).astype(F32).astype(BF16)
@@ -304,7 +309,10 @@
         [pltpu.VMEM(arg.shape, arg.dtype) for arg in fetched] + [pltpu.SemaphoreType.DMA((len(fetched),))],
         pltpu.HBM,
     )
-    near = lax.all_to_all(jnp.broadcast_to(block[None], (chips, ROWS, LANES)), group, 0, 0)
+    cores = [list(range(0, 2 * chips, 2)), [(n + chips) % (2 * chips) + 1 for n in range(0, 2 * chips, 2)]]
+    near = lax.all_to_all(
+        jnp.broadcast_to(block[None], (chips, ROWS, LANES)), group + ("side",), 0, 0, axis_index_groups=cores
+    )
     far = lax.ppermute(near, "side", swap)
     product, sums, norm, side = call(
         first_kernel,

time: 40.1 us -> 39.2 us (0.978)
  blocking collectives: 30 us -> 29.1 us
    all_to_all x1, blocking collectives: 18.8 us -> 16.9 us  [per_device(): lax.all_to_all(jnp.broadcast_to(block[None], (chips, ROWS, LANES)), group...]
    all_to_all x1, blocking collectives: 11.2 us -> 12.3 us  [per_device(): lax.all_to_all(copies, group + ('side',), 0, 0, tiled=True)]
where the time goes in v9:
time: 39.2 us; the launch traced here: 38.9 us
  blocking collectives  29.1 us (74%)
  Pallas kernels  7.47 us (19%)
  waiting for transfers between devices  0.83 us (2%)
  between operations  0.69 us (2%)
  starting transfers between devices  0.66 us (2%)
    all_to_all x1, blocking collectives, per_device(): lax.all_to_all(jnp.broadcast_to(block[None], (chips, ROWS, LANES)), group...  16.9 us
    all_to_all x1, blocking collectives, per_device(): lax.all_to_all(copies, group + ('side',), 0, 0, tiled=True)  12.3 us
    pallas_call x4, Pallas kernels, call(): pl.pallas_call(kernel, out_shape=tuple((jax.ShapeDtypeStruct(*out) for ou...  7.47 us
    ppermute x1, waiting for transfers between devices, per_device(): other = lax.ppermute(mine, 'side', swap)  0.83 us
  transfers between devices with their start and end apart: 2, of which 1 were waited for; matrix products, arithmetic and copies ran while one was open for 0% of the time, Pallas kernels for 5%

profile of v9, /device:TPU:0, one launch (start us, length us, event | category | flops | bytes accessed | tf_op | source)
XLA Modules:
  0.0 38.9 jit_solution(769425274743780127)
XLA Ops:
  0.6 1.1 %pack.1 = (bf16[72,128]{1,0:T(8,128)(2,1)S(1)}, f32[8,256]{1,0:T(8,128)S(1)}) custom-call(bf16[2,256]{1,0:T(2,128)(2,1)} %points_hbm.1, s32[1,256]{1,0:T(1,128)} %bitcast.6, f32[1,256]{1,0:T(1,128)} %bitcast.7, f32[32,256]{1,0:T(8,128)} %dir_ref.5), custom_call_target="tpu_custom_call" | custom-call | tf_op jit(solution)/shard_map/pack/pallas_call | solution.py:285
  1.8 0.0 copy-start
  1.8 0.0 copy-start.1
  1.8 16.9 %all_to_all.10.all_ref = bf16[16,72,128]{2,1,0:T(8,128)(2,1)S(1)} all-to-all(bf16[16,72,128]{2,1,0:T(8,128)(2,1)S(1)} %broadcast_in_dim.6), channel_id=1, replica_groups={{0,2,4,6,8,10,12,14,16,18,20,22,24,26,28,30},{17,19,21,23,25,27,29,31,1..., dimensions={0} | all-to-all | bytes 589824 | tf_op jit(solution)/shard_map/all_to_all | solution.py:313
  18.6 0.0 collective-permute-start
  18.6 0.0 copy-done
  18.6 0.0 copy-done.1
  18.6 1.9 %near_half.1 = (f32[32,256]{1,0:T(8,128)S(1)}, f32[40,256]{1,0:T(8,128)S(1)}, f32[32,128]{1,0:T(8,128)S(1)}, bf16[256,40]{1,0:T(8,128)(2,1)S(1)}) custom-call(f32[8,256]{1,0:T(8,128)S(1)} %get-tuple-element.11.own_ref, f32[32,256]{1,0:T(8,128)S(1)} %copy-done, f32[32,256]{1,0:T(8,128)S(1)} %copy-done.1, bf16[16,72,128]{2,1,0:T(8,128)(2,1)S(1)} %all_to_all.10.all_ref), custom_call_target="tpu_custom_call" | custom-call | tf_op jit(solution)/shard_map/near_half/pallas_call | solution.py:285
  20.5 0.0 collective-permute-done.all_ref
  20.5 1.9 %far_half.1 = (f32[32,256]{1,0:T(8,128)S(1)}, f32[6,4,128]{2,1,0:T(4,128)S(1)}) custom-call(f32[8,256]{1,0:T(8,128)S(1)} %get-tuple-element.11.own_ref, f32[32,256]{1,0:T(8,128)S(1)} %copy-done, f32[32,256]{1,0:T(8,128)S(1)} %copy-done.1, f32[32,128]{1,0:T(8,128)S(1)} %get-tuple-element.13.norm_ref, f32[32,256]{1,0:T(8,128)S(1)} %get-tuple-element.14.product_ref, ...), custom_call_target="tpu_custom_call" | custom-call | tf_op jit(solution)/shard_map/far_half/pallas_call | solution.py:285
  22.5 12.3 %all_to_all.11 = f32[32,3,4,128]{3,2,1,0:T(4,128)S(1)} all-to-all(f32[32,3,4,128]{3,2,1,0:T(4,128)S(1)} %bitcast.5), channel_id=1, replica_groups=mesh['row'=4,'pair'=4,'side'=2] {'row','pair','side'}, dimensions={0} | all-to-all | bytes 393216 | tf_op jit(solution)/shard_map/all_to_all | solution.py:330
  34.8 0.0 copy-start.2
  34.8 0.1 reduce_sum.9.mine_ref
  34.8 0.7 %collective-permute-start.1 = (f32[3,4,128]{2,1,0:T(4,128)S(1)}, f32[3,4,128]{2,1,0:T(4,128)S(1)}, u32[]{:S(2)}, u32[]{:S(2)}) collective-permute-start(f32[3,4,128]{2,1,0:T(4,128)S(1)} %reduce_sum.9.mine_ref), channel_id=1, source_target_pairs={{0,1},{1,0},{2,3},{3,2},{4,5},{5,4},{6,7},{7,6},{8,9},{9,8},{10,11... | collective-permute-start | bytes 18440 | tf_op jit(solution)/shard_map/ppermute | solution.py:331
  35.5 0.8 %collective-permute-done.1.other_ref = f32[3,4,128]{2,1,0:T(4,128)S(1)} collective-permute-done((f32[3,4,128]{2,1,0:T(4,128)S(1)}, f32[3,4,128]{2,1,0:T(4,128)S(1)}, u32[]{:S(2)}, u32[]{:S(2)}) %collective-permute-start.1) | collective-permute-done | bytes 6176 | tf_op jit(solution)/shard_map/ppermute | solution.py:331
  36.3 0.0 copy-done.2
  36.3 2.6 %final.1 = (f32[32,256]{1,0:T(8,128)}, f32[32,256]{1,0:T(8,128)}, f32[32,256]{1,0:T(8,128)}) custom-call(f32[3,4,128]{2,1,0:T(4,128)S(1)} %reduce_sum.9.mine_ref, f32[3,4,128]{2,1,0:T(4,128)S(1)} %collective-permute-done.1.other_ref, f32[32,256]{1,0:T(8,128)S(1)} %copy-done.2, f32[32,256]{1,0:T(8,128)S(1)} %copy-done.1, f32[32,256]{1,0:T(8,128)S(1)} %copy-done, ...), custom_call_target="tpu_custom_call" | custom-call | tf_op jit(solution)/shard_map/final/pallas_call | solution.py:285
  (2 shorter events, 0.1 us)
Async XLA Ops:
  1.8 16.9 %copy-start = (f32[32,256]{1,0:T(8,128)S(1)}, f32[32,256]{1,0:T(8,128)}, u32[]{:S(2)}) copy-start(f32[32,256]{1,0:T(8,128)} %dir_ref.5) | copy-start | bytes 98308
  1.8 16.9 %copy-start.1 = (f32[32,256]{1,0:T(8,128)S(1)}, f32[32,256]{1,0:T(8,128)}, u32[]{:S(2)}) copy-start(f32[32,256]{1,0:T(8,128)} %res_ref.5) | copy-start | bytes 98308
  18.6 1.9 %collective-permute-start = (bf16[16,72,128]{2,1,0:T(8,128)(2,1)S(1)}, bf16[16,72,128]{2,1,0:T(8,128)(2,1)S(1)}, u32[]{:S(2)}, u32[]{:S(2)}) collective-permute-start(bf16[16,72,128]{2,1,0:T(8,128)(2,1)S(1)} %all_to_all.10.all_ref), channel_id=1, source_target_pairs={{0,1},{1,0},{2,3},{3,2},{4,5},{5,4},{6,7},{7,6},{8,9},{9,8},{10,11... | collective-permute-start | bytes 884744 | tf_op jit(solution)/shard_map/ppermute | solution.py:316
  34.8 1.5 %copy-start.2 = (f32[32,256]{1,0:T(8,128)S(1)}, f32[32,256]{1,0:T(8,128)}, u32[]{:S(2)}) copy-start(f32[32,256]{1,0:T(8,128)} %sol_ref.1) | copy-start | bytes 98308
  34.8 1.5 %collective-permute-start.1 = (f32[3,4,128]{2,1,0:T(4,128)S(1)}, f32[3,4,128]{2,1,0:T(4,128)S(1)}, u32[]{:S(2)}, u32[]{:S(2)}) collective-permute-start(f32[3,4,128]{2,1,0:T(4,128)S(1)} %reduce_sum.9.mine_ref), channel_id=1, source_target_pairs={{0,1},{1,0},{2,3},{3,2},{4,5},{5,4},{6,7},{7,6},{8,9},{9,8},{10,11... | collective-permute-start | bytes 18440 | tf_op jit(solution)/shard_map/ppermute | solution.py:331

commit v10 on v8

--- a/solution.py
+++ b/solution.py
@@ -140,10 +140,15 @@
     return product, extra, sums[3 * rhs + 1 : 3 * rhs + 2]
 
 
+def place_in_group(chips):
+    place = lax.axis_index(("row", "pair"))
+    return jnp.where(lax.axis_index("side") == 0, place, (place + 3 * chips // 4) % chips)
+
+
 def first_kernel(own_ref, dir_ref, res_ref, all_ref, product_ref, sums_ref, norm_ref, side_ref):
     rhs, count = dir_ref.shape
     side_ref[...] = own_side(own_ref[...]).T.astype(BF16)
-    product, extra, number = half_product(lax.axis_index(("row", "pair")), own_ref, all_ref, side_ref)
+    product, extra, number = half_product(place_in_group(all_ref.shape[0]), own_ref, all_ref, side_ref)
     product_ref[...] = product
     labels = lax.broadcasted_iota(jnp.int32, (64, count), 0).astype(F32)
     onehot = (labels == own_ref[2:3, :]).astype(F32).astype(BF16)
@@ -315,7 +320,10 @@
         [pltpu.VMEM(arg.shape, arg.dtype) for arg in fetched] + [pltpu.SemaphoreType.DMA((len(fetched),))],
         pltpu.HBM,
     )
-    near = lax.all_to_all(jnp.broadcast_to(block[None], (chips, ROWS, LANES)), group, 0, 0)
+    cores = [list(range(0, 2 * chips, 2)), [(n + chips // 2) % (2 * chips) + 1 for n in range(0, 2 * chips, 2)]]
+    near = lax.all_to_all(
+        jnp.broadcast_to(block[None], (chips, ROWS, LANES)), group + ("side",), 0, 0, axis_index_groups=cores
+    )
     far = lax.ppermute(near, "side", swap)
     product, sums, norm, side = call(
         first_kernel,

time: 40 us -> 39.1 us (0.978)
  blocking collectives: 30 us -> 29.1 us
    all_to_all x1, blocking collectives: 18.8 us -> 17.9 us  [per_device(): lax.all_to_all(jnp.broadcast_to(block[None], (chips, ROWS, LANES)), group...]
where the time goes in v10:
time: 39.1 us; the launch traced here: 38.9 us
  blocking collectives  29.1 us (74%)
  Pallas kernels  7.41 us (19%)
  waiting for transfers between devices  0.83 us (2%)
  between operations  0.69 us (2%)
  starting transfers between devices  0.66 us (2%)
    all_to_all x1, blocking collectives, per_device(): lax.all_to_all(jnp.broadcast_to(block[None], (chips, ROWS, LANES)), group...  17.9 us
    all_to_all x1, blocking collectives, per_device(): lax.all_to_all(copies, group + ('side',), 0, 0, tiled=True)  11.2 us
    pallas_call x4, Pallas kernels, call(): pl.pallas_call(kernel, out_shape=tuple((jax.ShapeDtypeStruct(*out) for ou...  7.41 us
    ppermute x1, waiting for transfers between devices, per_device(): other = lax.ppermute(mine, 'side', swap)  0.83 us
  transfers between devices with their start and end apart: 2, of which 1 were waited for; matrix products, arithmetic and copies ran while one was open for 0% of the time, Pallas kernels for 5%

profile of v10, /device:TPU:0, one launch (start us, length us, event | category | flops | bytes accessed | tf_op | source)
XLA Modules:
  0.0 38.9 jit_solution(4836144707647079441)
XLA Ops:
  0.6 1.1 %pack.1 = (bf16[72,128]{1,0:T(8,128)(2,1)S(1)}, f32[8,256]{1,0:T(8,128)S(1)}) custom-call(bf16[2,256]{1,0:T(2,128)(2,1)} %points_hbm.1, s32[1,256]{1,0:T(1,128)} %bitcast.6, f32[1,256]{1,0:T(1,128)} %bitcast.7, f32[32,256]{1,0:T(8,128)} %dir_ref.5), custom_call_target="tpu_custom_call" | custom-call | tf_op jit(solution)/shard_map/pack/pallas_call | solution.py:296
  1.8 0.0 copy-start
  1.8 0.0 copy-start.1
  1.8 17.9 %all_to_all.10.all_ref = bf16[16,72,128]{2,1,0:T(8,128)(2,1)S(1)} all-to-all(bf16[16,72,128]{2,1,0:T(8,128)(2,1)S(1)} %broadcast_in_dim.6), channel_id=1, replica_groups={{0,2,4,6,8,10,12,14,16,18,20,22,24,26,28,30},{9,11,13,15,17,19,21,23,25..., dimensions={0} | all-to-all | bytes 589824 | tf_op jit(solution)/shard_map/all_to_all | solution.py:324
  19.7 0.0 collective-permute-start
  19.7 0.0 copy-done
  19.7 0.0 copy-done.1
  19.7 1.9 %near_half.1 = (f32[32,256]{1,0:T(8,128)S(1)}, f32[40,256]{1,0:T(8,128)S(1)}, f32[32,128]{1,0:T(8,128)S(1)}, bf16[256,40]{1,0:T(8,128)(2,1)S(1)}) custom-call(f32[8,256]{1,0:T(8,128)S(1)} %get-tuple-element.11.own_ref, f32[32,256]{1,0:T(8,128)S(1)} %copy-done, f32[32,256]{1,0:T(8,128)S(1)} %copy-done.1, bf16[16,72,128]{2,1,0:T(8,128)(2,1)S(1)} %all_to_all.10.all_ref), custom_call_target="tpu_custom_call" | custom-call | tf_op jit(solution)/shard_map/near_half/pallas_call | solution.py:296
  21.6 0.0 collective-permute-done.all_ref
  21.6 1.9 %far_half.1 = (f32[32,256]{1,0:T(8,128)S(1)}, f32[6,4,128]{2,1,0:T(4,128)S(1)}) custom-call(f32[8,256]{1,0:T(8,128)S(1)} %get-tuple-element.11.own_ref, f32[32,256]{1,0:T(8,128)S(1)} %copy-done, f32[32,256]{1,0:T(8,128)S(1)} %copy-done.1, f32[32,128]{1,0:T(8,128)S(1)} %get-tuple-element.13.norm_ref, f32[32,256]{1,0:T(8,128)S(1)} %get-tuple-element.14.product_ref, ...), custom_call_target="tpu_custom_call" | custom-call | tf_op jit(solution)/shard_map/far_half/pallas_call | solution.py:296
  23.5 11.2 %all_to_all.11 = f32[32,3,4,128]{3,2,1,0:T(4,128)S(1)} all-to-all(f32[32,3,4,128]{3,2,1,0:T(4,128)S(1)} %bitcast.5), channel_id=1, replica_groups=mesh['row'=4,'pair'=4,'side'=2] {'row','pair','side'}, dimensions={0} | all-to-all | bytes 393216 | tf_op jit(solution)/shard_map/all_to_all | solution.py:341
  34.8 0.0 copy-start.2
  34.8 0.1 reduce_sum.9.mine_ref
  34.8 0.7 %collective-permute-start.1 = (f32[3,4,128]{2,1,0:T(4,128)S(1)}, f32[3,4,128]{2,1,0:T(4,128)S(1)}, u32[]{:S(2)}, u32[]{:S(2)}) collective-permute-start(f32[3,4,128]{2,1,0:T(4,128)S(1)} %reduce_sum.9.mine_ref), channel_id=1, source_target_pairs={{0,1},{1,0},{2,3},{3,2},{4,5},{5,4},{6,7},{7,6},{8,9},{9,8},{10,11... | collective-permute-start | bytes 18440 | tf_op jit(solution)/shard_map/ppermute | solution.py:342
  35.5 0.8 %collective-permute-done.1.other_ref = f32[3,4,128]{2,1,0:T(4,128)S(1)} collective-permute-done((f32[3,4,128]{2,1,0:T(4,128)S(1)}, f32[3,4,128]{2,1,0:T(4,128)S(1)}, u32[]{:S(2)}, u32[]{:S(2)}) %collective-permute-start.1) | collective-permute-done | bytes 6176 | tf_op jit(solution)/shard_map/ppermute | solution.py:342
  36.3 0.0 copy-done.2
  36.3 2.5 %final.1 = (f32[32,256]{1,0:T(8,128)}, f32[32,256]{1,0:T(8,128)}, f32[32,256]{1,0:T(8,128)}) custom-call(f32[3,4,128]{2,1,0:T(4,128)S(1)} %reduce_sum.9.mine_ref, f32[3,4,128]{2,1,0:T(4,128)S(1)} %collective-permute-done.1.other_ref, f32[32,256]{1,0:T(8,128)S(1)} %copy-done.2, f32[32,256]{1,0:T(8,128)S(1)} %copy-done.1, f32[32,256]{1,0:T(8,128)S(1)} %copy-done, ...), custom_call_target="tpu_custom_call" | custom-call | tf_op jit(solution)/shard_map/final/pallas_call | solution.py:296
  (2 shorter events, 0.1 us)
Async XLA Ops:
  1.8 17.9 %copy-start = (f32[32,256]{1,0:T(8,128)S(1)}, f32[32,256]{1,0:T(8,128)}, u32[]{:S(2)}) copy-start(f32[32,256]{1,0:T(8,128)} %dir_ref.5) | copy-start | bytes 98308
  1.8 17.9 %copy-start.1 = (f32[32,256]{1,0:T(8,128)S(1)}, f32[32,256]{1,0:T(8,128)}, u32[]{:S(2)}) copy-start(f32[32,256]{1,0:T(8,128)} %res_ref.5) | copy-start | bytes 98308
  19.7 1.9 %collective-permute-start = (bf16[16,72,128]{2,1,0:T(8,128)(2,1)S(1)}, bf16[16,72,128]{2,1,0:T(8,128)(2,1)S(1)}, u32[]{:S(2)}, u32[]{:S(2)}) collective-permute-start(bf16[16,72,128]{2,1,0:T(8,128)(2,1)S(1)} %all_to_all.10.all_ref), channel_id=1, source_target_pairs={{0,1},{1,0},{2,3},{3,2},{4,5},{5,4},{6,7},{7,6},{8,9},{9,8},{10,11... | collective-permute-start | bytes 884744 | tf_op jit(solution)/shard_map/ppermute | solution.py:327
  34.8 1.5 %copy-start.2 = (f32[32,256]{1,0:T(8,128)S(1)}, f32[32,256]{1,0:T(8,128)}, u32[]{:S(2)}) copy-start(f32[32,256]{1,0:T(8,128)} %sol_ref.1) | copy-start | bytes 98308
  34.8 1.5 %collective-permute-start.1 = (f32[3,4,128]{2,1,0:T(4,128)S(1)}, f32[3,4,128]{2,1,0:T(4,128)S(1)}, u32[]{:S(2)}, u32[]{:S(2)}) collective-permute-start(f32[3,4,128]{2,1,0:T(4,128)S(1)} %reduce_sum.9.mine_ref), channel_id=1, source_target_pairs={{0,1},{1,0},{2,3},{3,2},{4,5},{5,4},{6,7},{7,6},{8,9},{9,8},{10,11... | collective-permute-start | bytes 18440 | tf_op jit(solution)/shard_map/ppermute | solution.py:342
